TPU v7x, 32 devices: a whole 2x2x4 slice. The times are simulated.
32 devices in a mesh: dp: 8 (over z, core), seq: 4 (over y, x).
Axes of the slice: x: 2, y: 2, z: 4, core: 2. Of those that a mesh axis runs over, the one named last changes fastest.
Arguments:
- hidden: bfloat16 [8, 2, 256, 8192], P('dp', None, 'seq'), may hold values from -6 to 6
- queries: bfloat16 [8, 2, 256, 4096], P('dp', None, 'seq'), may hold values from -240 to 240
- key_matrix: bfloat16 [8192, 1024], P('dp', 'seq'), may hold values from -0.0625 to 0.0625
- value_matrix: bfloat16 [8192, 1024], P('dp', 'seq'), may hold values from -0.0625 to 0.0625
- out_grad: bfloat16 [8, 2, 256, 4096], P('dp', None, 'seq'), may hold values from -6 to 6
Outputs:
- attn_out: bfloat16 [8, 2, 256, 4096], P('dp', None, 'seq')
- query_grad: bfloat16 [8, 2, 256, 4096], P('dp', None, 'seq')
- key_weight_grad: float32 [8192, 1024], P('dp', 'seq')
- value_weight_grad: float32 [8192, 1024], P('dp', 'seq')
All inputs are finite; a program needn't handle non-finite values.
Results may differ from a plain program's by a relative error of at most 0.025.
The roundings to bfloat16 on the way count: a program that leaves them out, or rounds other values in their place, can miss the bound.
Values may be sent and summed in bfloat16 or wider, within the bound.
A program may use at most 128 MiB of HBM per device.

v0:
```python
import functools
import math

import jax
import jax.numpy as jnp
import numpy as np
from jax import lax
from jax.experimental import pallas as pl
from jax.experimental.pallas import tpu as pltpu
from jax.sharding import PartitionSpec as P

HEAD_WIDTH = 128
ROPE_BASE = 500000.0
CORES = 2
MESH = pl.DeviceIdType.MESH
ANY = pl.BlockSpec(memory_space=pl.ANY)
VMEM = pl.BlockSpec(memory_space=pltpu.VMEM)
VMEM_LIMIT = 56 << 20


def grid_of(count):
    rows = 2 if count % 2 == 0 else 1
    return rows, count // rows


def place(n_seq, n_dp):
    dp, seq = lax.axis_index("dp"), lax.axis_index("seq")
    chips = n_dp // CORES
    chip, core = lax.div(dp, CORES), lax.rem(dp, CORES)
    rows, cols = grid_of(n_seq)
    row, col = lax.div(seq, cols), lax.rem(seq, cols)
    row_peers = [row * cols + lax.rem(col + d, cols) for d in range(1, cols)]
    col_peers = [lax.rem(row + d, rows) * cols + col for d in range(1, rows)]
    far_peers = [
        lax.rem(row + e, rows) * cols + lax.rem(col + d, cols)
        for e in range(1, rows)
        for d in range(1, cols)
    ]
    return dp, seq, chips, chip, core, row_peers, col_peers, far_peers


def greet(dp, seq, chips, chip, core, peers):
    barrier = pltpu.get_barrier_semaphore()
    ids = [(dp, p) for p in peers]
    ids.append((chip * CORES + 1 - core, seq))
    if chips > 1:
        for d in (1, chips - 1):
            ids.append((lax.rem(chip + d, chips) * CORES + core, seq))
    for device in ids:
        pl.semaphore_signal(barrier, inc=1, device_id=device, device_id_type=MESH)
    pl.semaphore_wait(barrier, len(ids))


def kernel(
    n_seq, n_dp, kv_heads, group, tile,
    hidden, queries, key_matrix, value_matrix, out_grad, cos, sin, cos_t, sin_t,
    attn_out, qgrad_out, key_grad, val_grad,
    hid, qry, grd, key_all, val_all, raw_both, keys, vals, attn, qgrad, pre_t,
    key_acc, val_acc, acc, mate_out, mate_in, chain_out, down_in, up_in,
    load_sem, own_sem, store_sem, hid_send, hid_recv, qry_send, qry_recv, grd_send, grd_recv,
    up_send, down_send, mate_w_send, w_recv, a_send, a_recv, q_send, q_recv,
    mate_send, mate_recv, chain_send, down_recv, up_recv,
):
    f32, bf16 = jnp.float32, jnp.bfloat16
    dp, seq, chips, chip, core, row_peers, col_peers, far_peers = place(n_seq, n_dp)
    peers = row_peers + col_peers + far_peers
    above, below = dp + CORES, dp - CORES
    mate = chip * CORES + 1 - core
    has_above, has_below = chip < chips - 1, chip > 0
    wide = group * HEAD_WIDTH
    width = kv_heads * wide
    total = keys.shape[0]
    half = HEAD_WIDTH // 2
    block = total // 2

    def head_cols(target, kv):
        return pl.ds(pl.multiple_of(target * width + kv * wide, wide), wide)

    def one_head(target, h):
        start = pl.multiple_of(target * width + h * HEAD_WIDTH, HEAD_WIDTH)
        return pl.ds(start, HEAD_WIDTH)

    loads = [
        (hidden, hid.at[:, seq], load_sem.at[0]),
        (key_matrix, key_all.at[dp], load_sem.at[1]),
        (value_matrix, val_all.at[dp], load_sem.at[2]),
    ]

    def own_loads(h):
        return (
            (queries.at[:, :, one_head(seq, h)], qry.at[h, :, seq], own_sem.at[0, h]),
            (out_grad.at[:, :, one_head(seq, h)], grd.at[h, :, seq], own_sem.at[1, h]),
        )

    greet(dp, seq, chips, chip, core, peers)
    sends = []
    slots = iter(range(hid_send.shape[0]))

    def send_hidden(source, part, target, src):
        copy = pltpu.make_async_remote_copy(
            src_ref=src, dst_ref=hid.at[part, source],
            send_sem=hid_send.at[next(slots)], recv_sem=hid_recv.at[source, part],
            device_id=(dp, target), device_id_type=MESH,
        )
        copy.start()
        sends.append(copy)

    def wait_hidden(source, part):
        pltpu.make_async_remote_copy(
            src_ref=hid.at[part, source], dst_ref=hid.at[part, source],
            send_sem=hid_send.at[0], recv_sem=hid_recv.at[source, part],
            device_id=(dp, source), device_id_type=MESH,
        ).wait_recv()

    tables = (key_all, val_all)
    owns = (key_matrix, value_matrix)

    def weight_copy(kind, piece, target_dp, send_sem, own=False):
        return pltpu.make_async_remote_copy(
            src_ref=owns[kind] if own else tables[kind].at[piece],
            dst_ref=tables[kind].at[piece],
            send_sem=send_sem, recv_sem=w_recv.at[piece, kind],
            device_id=(target_dp, seq), device_id_type=MESH,
        )

    def go(cond, copy_of, wait=False):
        @pl.when(cond)
        def _():
            copy = copy_of()
            copy.wait_send() if wait else copy.start()

    for p in row_peers:
        send_hidden(seq, 0, p, hidden.at[0])
    for p in col_peers:
        send_hidden(seq, 1, p, hidden.at[1])
    for kind in range(2):
        go(has_above, lambda: weight_copy(kind, dp, above, up_send.at[0, kind], True))
        go(has_below, lambda: weight_copy(kind, dp, below, down_send.at[0, kind], True))
    for p in row_peers:
        send_hidden(seq, 1, p, hidden.at[1])
    for p in col_peers:
        send_hidden(seq, 0, p, hidden.at[0])
    for kind in range(2):
        weight_copy(kind, dp, mate, mate_w_send.at[dp, kind], True).start()
    for copy in loads + [c for h in range(kv_heads * group) for c in own_loads(h)]:
        pltpu.make_async_copy(*copy).start()

    def relay_weight(step, kind):
        low, high = dp - CORES * step, dp + CORES * step

        @pl.when(chip >= step)
        def _():
            weight_copy(kind, low, below, up_send.at[step, kind]).wait_recv()
            go(has_above, lambda: weight_copy(kind, low, above, up_send.at[step, kind]))
            weight_copy(kind, low, mate, mate_w_send.at[low, kind]).start()

        @pl.when(chip + step < chips)
        def _():
            weight_copy(kind, high, above, down_send.at[step, kind]).wait_recv()
            go(has_below, lambda: weight_copy(kind, high, below, down_send.at[step, kind]))
            weight_copy(kind, high, mate, mate_w_send.at[high, kind]).start()

    def relay_hidden():
        for p in row_peers:
            wait_hidden(p, 0)
            for q in col_peers:
                send_hidden(p, 0, q, hid.at[0, p])
        for p in col_peers:
            wait_hidden(p, 1)
            for q in row_peers:
                send_hidden(p, 1, q, hid.at[1, p])

    def exchange(h, src, dst, send_sem, recv_sem):
        for i, p in enumerate(peers):
            copy = pltpu.make_async_remote_copy(
                src_ref=src.at[:, :, one_head(p, h)], dst_ref=dst.at[h, :, seq],
                send_sem=send_sem.at[h, i], recv_sem=recv_sem.at[h, seq],
                device_id=(dp, p), device_id_type=MESH,
            )
            copy.start()
            sends.append(copy)

    def wait_exchange(h, dst, send_sem, recv_sem):
        for p in peers:
            pltpu.make_async_remote_copy(
                src_ref=dst.at[h, :, p], dst_ref=dst.at[h, :, p],
                send_sem=send_sem.at[h, 0], recv_sem=recv_sem.at[h, p],
                device_id=(dp, p), device_id_type=MESH,
            ).wait_recv()

    if chips > 1:
        relay_weight(1, 0)
    relay_hidden()
    for h in range(kv_heads * group):
        exchange(h, queries, qry, qry_send, qry_recv)
        exchange(h, out_grad, grd, grd_send, grd_recv)
    if chips > 1:
        relay_weight(1, 1)
    for step in range(2, chips):
        for kind in range(2):
            relay_weight(step, kind)
    for p in row_peers:
        wait_hidden(p, 1)
    for p in col_peers:
        wait_hidden(p, 0)
    for p in far_peers:
        wait_hidden(p, 0)
        wait_hidden(p, 1)
    for other in range(chips):
        for kind in range(2):
            piece = other * CORES + 1 - core
            weight_copy(kind, piece, mate, mate_w_send.at[piece, kind]).wait_recv()
    for copy in loads:
        pltpu.make_async_copy(*copy).wait()

    deep = key_all.shape[1]

    def project(kv):
        lanes = pl.ds(kv * HEAD_WIDTH, HEAD_WIDTH)
        raw_both[...] = jnp.zeros_like(raw_both)

        @pl.loop(0, n_dp)
        def _(d):
            cols = pl.ds(pl.multiple_of(d * deep, deep), deep)
            rows = hid[:, :, :, cols].reshape(total, deep)
            both = jnp.concatenate([key_all[d, :, lanes], val_all[d, :, lanes]], axis=1)
            raw_both[...] += jnp.dot(rows, both, preferred_element_type=f32)

        raw = raw_both[:, :HEAD_WIDTH]
        swapped = jnp.concatenate([raw[:, half:], raw[:, :half]], axis=1)
        keys[:, lanes] = (raw * cos[...] + swapped * sin[...]).astype(bf16)
        vals[:, lanes] = raw_both[:, HEAD_WIDTH:].astype(bf16)

    scale = 1.0 / math.sqrt(HEAD_WIDTH)
    nt = (((1,), (1,)), ((), ()))
    tn = (((0,), (0,)), ((), ()))

    def attend(kv):
        lanes = pl.ds(kv * HEAD_WIDTH, HEAD_WIDTH)
        key_acc[...] = jnp.zeros_like(key_acc)
        val_acc[...] = jnp.zeros_like(val_acc)

        @pl.loop(0, group)
        def _(m):
            head = pl.ds(pl.multiple_of(m * HEAD_WIDTH, HEAD_WIDTH), HEAD_WIDTH)
            h = kv * group + m
            wait_exchange(h, qry, qry_send, qry_recv)
            wait_exchange(h, grd, grd_send, grd_recv)
            for copy in own_loads(h):
                pltpu.make_async_copy(*copy).wait()
            for b in range(2):
                span = (b + 1) * block
                q = qry[h, b].reshape(block, HEAD_WIDTH)
                g = grd[h, b].reshape(block, HEAD_WIDTH)
                k, v = keys[:span, lanes], vals[:span, lanes]
                s = lax.dot_general(q, k, nt, preferred_element_type=f32) * scale
                at = b * block + lax.broadcasted_iota(jnp.int32, s.shape, 0)
                col = lax.broadcasted_iota(jnp.int32, s.shape, 1)
                s = jnp.where(col <= at, s, -jnp.inf)
                e = jnp.exp(s - jnp.max(s, axis=1, keepdims=True))
                p = e * (1.0 / jnp.sum(e, axis=1, keepdims=True))
                p_half = p.astype(bf16)
                o = jnp.dot(p_half, v, preferred_element_type=f32).astype(bf16)
                attn[kv, b, :, :, head] = o.reshape(n_seq, block // n_seq, HEAD_WIDTH)
                dot = jnp.sum(g.astype(f32) * o.astype(f32), axis=1, keepdims=True)
                gp = lax.dot_general(g, v, nt, preferred_element_type=f32)
                ds = (p * (gp - dot) * scale).astype(bf16)
                dq = jnp.dot(ds, k, preferred_element_type=f32).astype(bf16)
                qgrad[kv, b, :, :, head] = dq.reshape(n_seq, block // n_seq, HEAD_WIDTH)
                key_acc[:, :span] += lax.dot_general(q, ds, tn, preferred_element_type=f32)
                val_acc[:, :span] += lax.dot_general(g, p_half, tn, preferred_element_type=f32)

        grown = key_acc[...]
        swapped = jnp.concatenate([grown[half:, :], grown[:half, :]], axis=0)
        pre_t[kv, :HEAD_WIDTH, :] = (grown * cos_t[...] - swapped * sin_t[...]).astype(bf16)
        pre_t[kv, HEAD_WIDTH:, :] = val_acc[...].astype(bf16)

    height, depth = acc.shape[2], acc.shape[3]
    results = ((attn, attn_out, a_send, a_recv), (qgrad, qgrad_out, q_send, q_recv))

    def own_store(kv, which):
        src, dst, _, _ = results[which]
        return pltpu.make_async_copy(
            src.at[kv, :, seq], dst.at[:, :, head_cols(seq, kv)], store_sem.at[which, kv]
        )

    def give_back(kv):
        for which, (src, dst, send_sem, recv_sem) in enumerate(results):
            for i, p in enumerate(peers):
                copy = pltpu.make_async_remote_copy(
                    src_ref=src.at[kv, :, p], dst_ref=dst.at[:, :, head_cols(seq, kv)],
                    send_sem=send_sem.at[kv, i], recv_sem=recv_sem.at[kv, seq],
                    device_id=(dp, p), device_id_type=MESH,
                )
                copy.start()
                sends.append(copy)
            own_store(kv, which).start()

    def wait_back(kv):
        for which, (src, dst, send_sem, recv_sem) in enumerate(results):
            for p in peers:
                pltpu.make_async_remote_copy(
                    src_ref=src.at[kv, :, p], dst_ref=dst.at[:, :, head_cols(p, kv)],
                    send_sem=send_sem.at[kv, 0], recv_sem=recv_sem.at[kv, p],
                    device_id=(dp, p), device_id_type=MESH,
                ).wait_recv()
            own_store(kv, which).wait()

    def mate_copy(kv, t):
        return pltpu.make_async_remote_copy(
            src_ref=mate_out.at[kv, t], dst_ref=mate_in.at[kv, t],
            send_sem=mate_send.at[kv, t], recv_sem=mate_recv.at[kv, t],
            device_id=(mate, seq), device_id_type=MESH,
        )

    def chain_copy(kv, t, down):
        return pltpu.make_async_remote_copy(
            src_ref=chain_out.at[kv, t], dst_ref=(down_in if down else up_in).at[kv, t],
            send_sem=chain_send.at[kv, t], recv_sem=(down_recv if down else up_recv).at[kv, t],
            device_id=(below if down else above, seq), device_id_type=MESH,
        )

    def product(kv, which, store):
        @pl.loop(0, depth // tile)
        def _(i):
            cols = pl.ds(pl.multiple_of(which * depth + i * tile, tile), tile)
            rows = hid[:, :, :, cols].reshape(total, tile)
            part = jnp.dot(pre_t[kv], rows, preferred_element_type=f32)
            store(pl.ds(pl.multiple_of(i * tile, tile), tile), part)

    strip = 32

    def sweep(fn):
        @pl.loop(0, height // strip)
        def _(i):
            fn(pl.ds(pl.multiple_of(i * strip, strip), strip))

    def relay(kv, t, down, has_input):
        mate_copy(kv, t).wait_recv()

        def merge(extra):
            def fn(rows):
                v = acc[kv, t, rows, :]
                for e in (mate_in,) + extra:
                    v = v + e[kv, t, rows, :].astype(f32)
                chain_out[kv, t, rows, :] = v.astype(bf16)

            sweep(fn)

        if has_input:
            chain_copy(kv, t, down).wait_recv()
            merge((down_in if down else up_in,))
        else:
            merge(())
        chain_copy(kv, t, down).start()

    is_end = jnp.logical_or(chip == 0, chip == chips - 1)

    flip = lax.div(chips - 1 - chip, max(chips - 1, 1)) if chips > 1 else 0

    def turn(i):
        odd, k = lax.rem(i, 2), lax.div(i, 2)
        t = odd * (chips - 1 - k) + (1 - odd) * k
        return flip * (chips - 1 - t) + (1 - flip) * t

    def early(kv, t):
        @pl.when(jnp.logical_and(chip == chips - 1, t < chip))
        def _():
            relay(kv, t, True, False)

        @pl.when(jnp.logical_and(chip == 0, t > chip))
        def _():
            relay(kv, t, False, False)

    def products(kv):
        @pl.loop(0, chips)
        def _(i):
            t = turn(i)

            def to_mate(cols, part):
                mate_out[kv, t, :, cols] = part.astype(bf16)

            def to_acc(cols, part):
                acc[kv, t, :, cols] = part

            product(kv, t * CORES + 1 - core, to_mate)
            mate_copy(kv, t).start()
            product(kv, t * CORES + core, to_acc)

            @pl.when(i > 0)
            def _():
                early(kv, turn(i - 1))

        early(kv, turn(chips - 1))

    def chain(kv, cond):
        @pl.when(cond)
        def _():
            @pl.loop(0, chips - 1)
            def _(tau):
                k_down = tau - (chips - 1 - chip)
                k_up = tau - chip

                @pl.when(jnp.logical_and(k_down >= 0, k_down < chip))
                def _():
                    relay(kv, k_down, True, True)

                @pl.when(jnp.logical_and(k_up >= 0, k_up < chips - 1 - chip))
                def _():
                    relay(kv, chips - 1 - k_up, False, True)

    def prepare(kv):
        mate_copy(kv, chip).wait_recv()

        def fn(rows):
            acc[kv, chip, rows, :] += mate_in[kv, chip, rows, :].astype(f32)

        sweep(fn)

    def finish(kv):
        lanes = pl.ds(kv * HEAD_WIDTH, HEAD_WIDTH)

        def put(extra):
            @pl.loop(0, depth // HEAD_WIDTH)
            def _(j):
                at = pl.ds(pl.multiple_of(j * HEAD_WIDTH, HEAD_WIDTH), HEAD_WIDTH)
                v = acc[kv, chip, :, at]
                for e in extra:
                    v = v + e[kv, chip, :, at].astype(f32)
                key_grad[at, lanes] = v[:HEAD_WIDTH, :].T
                val_grad[at, lanes] = v[HEAD_WIDTH:, :].T

        if chips == 1:
            put(())
            return

        @pl.when(has_above)
        def _():
            chain_copy(kv, chip, True).wait_recv()

        @pl.when(has_below)
        def _():
            chain_copy(kv, chip, False).wait_recv()

        @pl.when(chip == 0)
        def _():
            put((down_in,))

        @pl.when(chip == chips - 1)
        def _():
            put((up_in,))

        @pl.when(jnp.logical_not(is_end))
        def _():
            put((down_in, up_in))

    for kv in range(kv_heads):
        project(kv)
        attend(kv)
        products(kv)
        give_back(kv)
    for kv in range(kv_heads):
        prepare(kv)
        chain(kv, jnp.logical_not(is_end))
    for kv in range(kv_heads):
        wait_back(kv)
        finish(kv)
    for copy in sends:
        copy.wait_send()
    for kind in range(2):
        for step in range(max(chips - 1, 1)):
            low, high = dp - CORES * step, dp + CORES * step
            go(jnp.logical_and(has_above, chip >= step),
               lambda: weight_copy(kind, low, above, up_send.at[step, kind]), True)
            go(jnp.logical_and(has_below, chip + step < chips),
               lambda: weight_copy(kind, high, below, down_send.at[step, kind]), True)
        for other in range(chips):
            piece = other * CORES + core
            weight_copy(kind, piece, mate, mate_w_send.at[piece, kind]).wait_send()
    for kv in range(kv_heads):
        for t in range(chips):
            mate_copy(kv, t).wait_send()
            go(chip != t, lambda: chain_copy(kv, t, True), True)


def put_kernel(*refs):
    count = len(refs) // 2
    sem = refs[-1]
    copies = [
        pltpu.make_async_copy(refs[i], refs[count + i], sem.at[i]) for i in range(count)
    ]
    for copy in copies:
        copy.start()
    for copy in copies:
        copy.wait()


def put_all(*arrays):
    return pl.pallas_call(
        put_kernel,
        out_shape=[jax.ShapeDtypeStruct(x.shape, x.dtype) for x in arrays],
        in_specs=[pl.BlockSpec(memory_space=pltpu.VMEM)] * len(arrays),
        out_specs=[ANY] * len(arrays),
        scratch_shapes=[pltpu.SemaphoreType.DMA((len(arrays),))],
        compiler_params=pltpu.CompilerParams(vmem_limit_bytes=1 << 20),
        name="put_all",
    )(*arrays)


def local(n_seq, n_dp, hidden, queries, key_matrix, value_matrix, out_grad):
    _, stretches, tokens, embed = hidden.shape
    full = queries.shape[3]
    width = full // n_seq
    deep, kv_width = key_matrix.shape
    kv_heads = kv_width // HEAD_WIDTH
    group = width // kv_width
    wide = group * HEAD_WIDTH
    chips = n_dp // CORES
    rows, cols = grid_of(n_seq)
    hid_sends = 2 * (rows - 1 + cols - 1) + 2 * (rows - 1) * (cols - 1)
    total = stretches * n_seq * tokens
    bf16, f32 = jnp.bfloat16, jnp.float32
    dma = pltpu.SemaphoreType.DMA
    half = HEAD_WIDTH // 2
    inverse = np.exp(
        np.arange(half, dtype=np.float32) * np.float32(-2.0 * math.log(ROPE_BASE) / HEAD_WIDTH)
    ).astype(np.float32)
    phase = np.arange(total, dtype=np.float32)[:, None] * inverse[None, :]
    cos_half, sin_half = np.cos(phase), np.sin(phase)
    cos = np.concatenate([cos_half, cos_half], axis=1).astype(np.float32)
    sin = np.concatenate([-sin_half, sin_half], axis=1).astype(np.float32)
    heads = (kv_heads, stretches, n_seq, tokens, wide)
    single = (kv_heads * group, stretches, n_seq, tokens, HEAD_WIDTH)
    height = 2 * HEAD_WIDTH
    blocks = (kv_heads, chips, height, deep)
    weights = (n_dp, deep, kv_width)
    attn_out, query_grad, key_grad, val_grad = pl.pallas_call(
        functools.partial(kernel, n_seq, n_dp, kv_heads, group, math.gcd(deep, 256)),
        out_shape=[
            pltpu.VMEM((stretches, tokens, full), bf16),
            pltpu.VMEM((stretches, tokens, full), bf16),
            pltpu.VMEM((deep, kv_width), f32),
            pltpu.VMEM((deep, kv_width), f32),
        ],
        in_specs=[ANY] * 5 + [VMEM] * 4,
        out_specs=[VMEM] * 4,
        scratch_shapes=[
            pltpu.VMEM((stretches, n_seq, tokens, embed), bf16),
            pltpu.VMEM(single, bf16),
            pltpu.VMEM(single, bf16),
            pltpu.VMEM(weights, bf16),
            pltpu.VMEM(weights, bf16),
            pltpu.VMEM((total, 2 * HEAD_WIDTH), f32),
            pltpu.VMEM((total, kv_width), bf16),
            pltpu.VMEM((total, kv_width), bf16),
            pltpu.VMEM(heads, bf16),
            pltpu.VMEM(heads, bf16),
            pltpu.VMEM((kv_heads, height, total), bf16),
            pltpu.VMEM((HEAD_WIDTH, total), f32),
            pltpu.VMEM((HEAD_WIDTH, total), f32),
            pltpu.VMEM(blocks, f32),
            pltpu.VMEM(blocks, bf16),
            pltpu.VMEM(blocks, bf16),
            pltpu.VMEM(blocks, bf16),
            pltpu.VMEM(blocks, bf16),
            pltpu.VMEM(blocks, bf16),
            dma((3,)), dma((2, kv_heads * group)), dma((2, kv_heads)),
            dma((hid_sends,)), dma((n_seq, 2)),
            dma((kv_heads * group, n_seq)), dma((kv_heads * group, n_seq)),
            dma((kv_heads * group, n_seq)), dma((kv_heads * group, n_seq)),
            dma((chips, 2)), dma((chips, 2)), dma((n_dp, 2)), dma((n_dp, 2)),
            dma((kv_heads, n_seq)), dma((kv_heads, n_seq)),
            dma((kv_heads, n_seq)), dma((kv_heads, n_seq)),
            dma((kv_heads, chips)), dma((kv_heads, chips)), dma((kv_heads, chips)),
            dma((kv_heads, chips)), dma((kv_heads, chips)),
        ],
        compiler_params=pltpu.CompilerParams(
            collective_id=0, has_side_effects=True, vmem_limit_bytes=VMEM_LIMIT
        ),
        name="attention_step",
    )(hidden[0], queries[0], key_matrix, value_matrix, out_grad[0],
      cos, sin, cos.T.copy(), sin.T.copy())
    attn_out, query_grad, key_grad, val_grad = put_all(
        attn_out, query_grad, key_grad, val_grad
    )
    return attn_out[None], query_grad[None], key_grad, val_grad


def solution(mesh):
    n_dp, n_seq = mesh.shape["dp"], mesh.shape["seq"]
    tokens, weights = P("dp", None, "seq", None), P("dp", "seq")
    return jax.shard_map(
        functools.partial(local, n_seq, n_dp),
        mesh=mesh,
        in_specs=(tokens, tokens, weights, weights, tokens),
        out_specs=(tokens, tokens, weights, weights),
        check_vma=False,
    )
```

profile of v0, /device:TPU:0, one launch (start us, length us, event | category | flops | bytes accessed | tf_op | source)
XLA Modules:
  0.0 166.9 jit_solution(13400961125249923602)
XLA Ops:
  0.6 164.2 %attention_step.1 = (bf16[2,64,4096]{2,1,0:T(8,128)(2,1)S(1)}, bf16[2,64,4096]{2,1,0:T(8,128)(2,1)S(1)}, f32[1024,256]{1,0:T(8,128)S(1)}, f32[1024,256]{1,0:T(8,128)S(1)}) custom-call(bf16[2,64,8192]{2,1,0:T(8,128)(2,1)} %bitcast.5, bf16[2,64,4096]{2,1,0:T(8,128)(2,1)} %bitcast.6, bf16[1024,256]{1,0:T(8,128)(2,1)} %key_matrix.1, ...), custom_call_target="tpu_custom_call" | custom-call | tf_op jit(solution)/shard_map/attention_step/pallas_call | solution.py:537
  164.9 2.0 %put_all.1 = (bf16[2,64,4096]{2,1,0:T(8,128)(2,1)}, bf16[2,64,4096]{2,1,0:T(8,128)(2,1)}, f32[1024,256]{1,0:T(8,128)}, f32[1024,256]{1,0:T(8,128)}) custom-call(bf16[2,64,4096]{2,1,0:T(8,128)(2,1)S(1)} %get-tuple-element.12.refs_0_, bf16[2,64,4096]{2,1,0:T(8,128)(2,1)S(1)} %get-tuple-element.13.refs_1_, f32[1024,256]{1,0:T(8,128)S(1)} %get-tuple-element.14.refs_2_, ...), custom_call_target="tpu_custom_call" | custom-call | tf_op jit(solution)/shard_map/put_all/pallas_call | solution.py:499
where the time goes:
time: 167 us
  Pallas kernels  166 us (99%)
    pallas_call x1, Pallas kernels, local(): pl.pallas_call(functools.partial(kernel, n_seq, n_dp, kv_heads, group, ma...  164 us

commit v1 on v0

v1 whole, which is shorter than its diff:
```python
import functools
import math

import jax
import jax.numpy as jnp
import numpy as np
from jax import lax
from jax.experimental import pallas as pl
from jax.experimental.pallas import tpu as pltpu
from jax.sharding import PartitionSpec as P

HEAD_WIDTH = 128
ROPE_BASE = 500000.0
CORES = 2
MESH = pl.DeviceIdType.MESH
ANY = pl.BlockSpec(memory_space=pl.ANY)
VMEM = pl.BlockSpec(memory_space=pltpu.VMEM)
VMEM_LIMIT = 56 << 20


def grid_of(count):
    rows = 2 if count % 2 == 0 else 1
    return rows, count // rows


def place(n_seq, n_dp):
    dp, seq = lax.axis_index("dp"), lax.axis_index("seq")
    chips = n_dp // CORES
    chip, core = lax.div(dp, CORES), lax.rem(dp, CORES)
    rows, cols = grid_of(n_seq)
    row, col = lax.div(seq, cols), lax.rem(seq, cols)
    row_peers = [row * cols + lax.rem(col + d, cols) for d in range(1, cols)]
    col_peers = [lax.rem(row + d, rows) * cols + col for d in range(1, rows)]
    far_peers = [
        lax.rem(row + e, rows) * cols + lax.rem(col + d, cols)
        for e in range(1, rows)
        for d in range(1, cols)
    ]
    return dp, seq, chips, chip, core, row_peers, col_peers, far_peers


def kernel(
    n_seq, n_dp, kv_heads, group, tile,
    hidden, queries, key_matrix, value_matrix, out_grad, cos, sin, cos_t, sin_t,
    attn_out, qgrad_out, key_grad, val_grad,
    hid, qry, grd, key_all, val_all, raw_k, raw_v, own_k, own_v, out_k, out_v, in_k, in_v,
    keys, vals, attn, qgrad, pre_t, pre_in,
    key_acc, val_acc, acc, mate_out, mate_in, far_out, far_in,
    load_sem, own_sem, store_sem, hid_send, hid_recv, qry_send, qry_recv, grd_send, grd_recv,
    far_w_send, mate_w_send, w_recv, k_send, k_recv, v_send, v_recv, pre_send, pre_recv,
    a_send, a_recv, q_send, q_recv, mate_send, mate_recv, far_send, far_recv,
):
    f32, bf16 = jnp.float32, jnp.bfloat16
    dp, seq, chips, chip, core, row_peers, col_peers, far_peers = place(n_seq, n_dp)
    peers = row_peers + col_peers + far_peers
    near = chips // 2
    side, slot_w = lax.div(chip, near), lax.rem(chip, near)
    mate = chip * CORES + 1 - core
    twin = ((1 - side) * near + slot_w) * CORES + core
    others = [lax.rem(slot_w + d, near) for d in range(1, near)]

    def owner(w):
        return (side * near + w) * CORES + core

    wide = group * HEAD_WIDTH
    width = kv_heads * wide
    total = keys.shape[0]
    half = HEAD_WIDTH // 2
    block = total // 2
    deep = key_all.shape[1]
    quarter = hid.shape[-1]
    per = quarter // deep
    mine = slot_w * CORES + core

    barrier = pltpu.get_barrier_semaphore()
    greeted = [(dp, p) for p in peers] + [(mate, seq), (twin, seq)]
    greeted += [(owner(w), seq) for w in others]
    for device in greeted:
        pl.semaphore_signal(barrier, inc=1, device_id=device, device_id_type=MESH)
    pl.semaphore_wait(barrier, len(greeted))

    def head_cols(target, kv):
        return pl.ds(pl.multiple_of(target * width + kv * wide, wide), wide)

    def one_head(target, h):
        start = pl.multiple_of(target * width + h * HEAD_WIDTH, HEAD_WIDTH)
        return pl.ds(start, HEAD_WIDTH)

    def embed_cols(which, j):
        return pl.ds(pl.multiple_of((which * 2 + j) * quarter, quarter), quarter)

    loads = [
        (hidden.at[:, :, embed_cols(side, j)], hid.at[0, j, :, seq], load_sem.at[j])
        for j in range(2)
    ] + [
        (key_matrix, key_all.at[mine], load_sem.at[2]),
        (value_matrix, val_all.at[mine], load_sem.at[3]),
    ]

    def own_loads(h):
        return (
            (queries.at[:, :, one_head(seq, h)], qry.at[h, :, seq], own_sem.at[0, h]),
            (out_grad.at[:, :, one_head(seq, h)], grd.at[h, :, seq], own_sem.at[1, h]),
        )

    sends = []

    def start(copy):
        copy.start()
        sends.append(copy)

    slots = iter(range(hid_send.shape[0]))

    def hidden_copy(slot, e, j, source, target_dp, target, src, send_sem):
        return pltpu.make_async_remote_copy(
            src_ref=src, dst_ref=hid.at[slot, j, e, source],
            send_sem=send_sem, recv_sem=hid_recv.at[slot, e, j, source],
            device_id=(target_dp, target), device_id_type=MESH,
        )

    def send_hidden(slot, e, j, source, target, own=False):
        src = hidden.at[e, :, embed_cols(side, j)] if own else hid.at[slot, j, e, source]
        start(hidden_copy(slot, e, j, source, dp, target, src, hid_send.at[next(slots)]))

    def wait_hidden(slot, e, j, source):
        src = hid.at[slot, j, e, source]
        hidden_copy(slot, e, j, source, dp, source, src, hid_send.at[0]).wait_recv()

    def direct(slot, e):
        own = slot == 0
        for first, second, j_pair in ((row_peers, col_peers, (0, 1)), (row_peers, col_peers, (1, 0))):
            for p in first:
                send_hidden(slot, e, j_pair[0], seq, p, own)
            for p in second:
                send_hidden(slot, e, j_pair[1], seq, p, own)

    def relay_hidden(slot, e):
        for p in row_peers:
            wait_hidden(slot, e, 0, p)
            for q in col_peers:
                send_hidden(slot, e, 0, p, q)
        for p in col_peers:
            wait_hidden(slot, e, 1, p)
            for q in row_peers:
                send_hidden(slot, e, 1, p, q)

    def wait_rest(slot, e):
        for p in row_peers:
            wait_hidden(slot, e, 1, p)
        for p in col_peers:
            wait_hidden(slot, e, 0, p)
        for p in far_peers:
            wait_hidden(slot, e, 0, p)
            wait_hidden(slot, e, 1, p)

    def arrive(e):
        for j in range(2):
            src = hid.at[1, j, e, seq]
            hidden_copy(1, e, j, seq, twin, seq, src, hid_send.at[0]).wait_recv()

    tables = (key_all, val_all)
    owns = (key_matrix, value_matrix)

    def weight_copy(kind, piece, target_dp, send_sem, own=False):
        return pltpu.make_async_remote_copy(
            src_ref=owns[kind] if own else tables[kind].at[piece],
            dst_ref=tables[kind].at[piece],
            send_sem=send_sem, recv_sem=w_recv.at[piece, kind],
            device_id=(target_dp, seq), device_id_type=MESH,
        )

    def relay_weights():
        for i, w in enumerate(others):
            for kind in range(2):
                piece = w * CORES + core
                weight_copy(kind, piece, owner(w), far_w_send.at[i, kind]).wait_recv()
                start(weight_copy(kind, piece, mate, mate_w_send.at[i + 1, kind]))

    def wait_weights():
        for w in [slot_w] + others:
            for kind in range(2):
                piece = w * CORES + 1 - core
                weight_copy(kind, piece, mate, mate_w_send.at[0, kind]).wait_recv()

    def exchange(h, src, dst, send_sem, recv_sem):
        for i, p in enumerate(peers):
            start(pltpu.make_async_remote_copy(
                src_ref=src.at[:, :, one_head(p, h)], dst_ref=dst.at[h, :, seq],
                send_sem=send_sem.at[h, i], recv_sem=recv_sem.at[h, seq],
                device_id=(dp, p), device_id_type=MESH,
            ))

    def wait_exchange(h, dst, send_sem, recv_sem):
        for p in peers:
            pltpu.make_async_remote_copy(
                src_ref=dst.at[h, :, p], dst_ref=dst.at[h, :, p],
                send_sem=send_sem.at[h, 0], recv_sem=recv_sem.at[h, p],
                device_id=(dp, p), device_id_type=MESH,
            ).wait_recv()

    def project(slot, e):
        raw_k[...] = jnp.zeros_like(raw_k)
        raw_v[...] = jnp.zeros_like(raw_v)

        @pl.loop(0, 2 * per)
        def _(i):
            j, at = lax.div(i, per), lax.rem(i, per)
            cols = pl.ds(pl.multiple_of(at * deep, deep), deep)
            rows = hid[slot, j, e, :, :, cols].reshape(block, deep)
            raw_k[...] += jnp.dot(rows, key_all[i], preferred_element_type=f32)
            raw_v[...] += jnp.dot(rows, val_all[i], preferred_element_type=f32)

        for kv in range(kv_heads):
            lanes = pl.ds(kv * HEAD_WIDTH, HEAD_WIDTH)
            to_k, to_v = (own_k, own_v) if slot == 0 else (out_k, out_v)
            to_k[kv, e] = raw_k[:, lanes].astype(to_k.dtype)
            to_v[kv, e] = raw_v[:, lanes].astype(to_v.dtype)

    def raw_copies(kv, e):
        return [
            pltpu.make_async_remote_copy(
                src_ref=src.at[kv, e], dst_ref=dst.at[kv, e],
                send_sem=send_sem.at[kv, e], recv_sem=recv_sem.at[kv, e],
                device_id=(twin, seq), device_id_type=MESH,
            )
            for src, dst, send_sem, recv_sem in (
                (out_k, in_k, k_send, k_recv), (out_v, in_v, v_send, v_recv),
            )
        ]

    def send_raw(e):
        for kv in range(kv_heads):
            for copy in raw_copies(kv, e):
                start(copy)

    def settle(kv, e):
        lanes = pl.ds(kv * HEAD_WIDTH, HEAD_WIDTH)
        rows = pl.ds(e * block, block)
        for copy in raw_copies(kv, e):
            copy.wait_recv()
        raw = own_k[kv, e] + in_k[kv, e]
        swapped = jnp.concatenate([raw[:, half:], raw[:, :half]], axis=1)
        keys[rows, lanes] = (raw * cos[rows, :] + swapped * sin[rows, :]).astype(bf16)
        vals[rows, lanes] = (own_v[kv, e] + in_v[kv, e].astype(f32)).astype(bf16)

    scale = 1.0 / math.sqrt(HEAD_WIDTH)
    nt = (((1,), (1,)), ((), ()))
    tn = (((0,), (0,)), ((), ()))

    def attend(kv):
        lanes = pl.ds(kv * HEAD_WIDTH, HEAD_WIDTH)
        key_acc[...] = jnp.zeros_like(key_acc)
        val_acc[...] = jnp.zeros_like(val_acc)

        @pl.loop(0, group)
        def _(m):
            head = pl.ds(pl.multiple_of(m * HEAD_WIDTH, HEAD_WIDTH), HEAD_WIDTH)
            h = kv * group + m
            wait_exchange(h, qry, qry_send, qry_recv)
            wait_exchange(h, grd, grd_send, grd_recv)
            for copy in own_loads(h):
                pltpu.make_async_copy(*copy).wait()
            for b in range(2):
                span = (b + 1) * block
                q = qry[h, b].reshape(block, HEAD_WIDTH)
                g = grd[h, b].reshape(block, HEAD_WIDTH)
                k, v = keys[:span, lanes], vals[:span, lanes]
                s = lax.dot_general(q, k, nt, preferred_element_type=f32) * scale
                at = b * block + lax.broadcasted_iota(jnp.int32, s.shape, 0)
                col = lax.broadcasted_iota(jnp.int32, s.shape, 1)
                s = jnp.where(col <= at, s, -jnp.inf)
                e = jnp.exp(s - jnp.max(s, axis=1, keepdims=True))
                p = e * (1.0 / jnp.sum(e, axis=1, keepdims=True))
                p_half = p.astype(bf16)
                o = jnp.dot(p_half, v, preferred_element_type=f32).astype(bf16)
                attn[kv, b, :, :, head] = o.reshape(n_seq, block // n_seq, HEAD_WIDTH)
                dot = jnp.sum(g.astype(f32) * o.astype(f32), axis=1, keepdims=True)
                gp = lax.dot_general(g, v, nt, preferred_element_type=f32)
                ds = (p * (gp - dot) * scale).astype(bf16)
                dq = jnp.dot(ds, k, preferred_element_type=f32).astype(bf16)
                qgrad[kv, b, :, :, head] = dq.reshape(n_seq, block // n_seq, HEAD_WIDTH)
                key_acc[:, :span] += lax.dot_general(q, ds, tn, preferred_element_type=f32)
                val_acc[:, :span] += lax.dot_general(g, p_half, tn, preferred_element_type=f32)

        grown = key_acc[...]
        swapped = jnp.concatenate([grown[half:, :], grown[:half, :]], axis=0)
        pre_t[kv, :HEAD_WIDTH, :] = (grown * cos_t[...] - swapped * sin_t[...]).astype(bf16)
        pre_t[kv, HEAD_WIDTH:, :] = val_acc[...].astype(bf16)

    def pre_copy(kv):
        return pltpu.make_async_remote_copy(
            src_ref=pre_t.at[kv], dst_ref=pre_in.at[kv],
            send_sem=pre_send.at[kv], recv_sem=pre_recv.at[kv],
            device_id=(twin, seq), device_id_type=MESH,
        )

    height, depth = acc.shape[2], acc.shape[3]
    results = ((attn, attn_out, a_send, a_recv), (qgrad, qgrad_out, q_send, q_recv))

    def own_store(kv, which):
        src, dst, _, _ = results[which]
        return pltpu.make_async_copy(
            src.at[kv, :, seq], dst.at[:, :, head_cols(seq, kv)], store_sem.at[which, kv]
        )

    def give_back(kv):
        for which, (src, dst, send_sem, recv_sem) in enumerate(results):
            for i, p in enumerate(peers):
                start(pltpu.make_async_remote_copy(
                    src_ref=src.at[kv, :, p], dst_ref=dst.at[:, :, head_cols(seq, kv)],
                    send_sem=send_sem.at[kv, i], recv_sem=recv_sem.at[kv, seq],
                    device_id=(dp, p), device_id_type=MESH,
                ))
            own_store(kv, which).start()

    def wait_back(kv):
        for which, (src, dst, send_sem, recv_sem) in enumerate(results):
            for p in peers:
                pltpu.make_async_remote_copy(
                    src_ref=src.at[kv, :, p], dst_ref=dst.at[:, :, head_cols(p, kv)],
                    send_sem=send_sem.at[kv, 0], recv_sem=recv_sem.at[kv, p],
                    device_id=(dp, p), device_id_type=MESH,
                ).wait_recv()
            own_store(kv, which).wait()

    def mate_copy(kv, w):
        return pltpu.make_async_remote_copy(
            src_ref=mate_out.at[kv, w], dst_ref=mate_in.at[kv, w],
            send_sem=mate_send.at[kv, w], recv_sem=mate_recv.at[kv, w],
            device_id=(mate, seq), device_id_type=MESH,
        )

    def far_copy(kv, i, w):
        return pltpu.make_async_remote_copy(
            src_ref=far_out.at[kv, i], dst_ref=far_in.at[kv, slot_w],
            send_sem=far_send.at[kv, i], recv_sem=far_recv.at[kv, slot_w],
            device_id=(owner(w), seq), device_id_type=MESH,
        )

    def wait_far(kv, i, w):
        pltpu.make_async_remote_copy(
            src_ref=far_out.at[kv, i], dst_ref=far_in.at[kv, w],
            send_sem=far_send.at[kv, i], recv_sem=far_recv.at[kv, w],
            device_id=(owner(w), seq), device_id_type=MESH,
        ).wait_recv()

    def product(kv, piece, store):
        j, at = lax.div(piece, per), lax.rem(piece, per)

        @pl.loop(0, depth // tile)
        def _(i):
            cols = pl.ds(pl.multiple_of(at * depth + i * tile, tile), tile)
            part = jnp.dot(
                pre_t[kv], hid[0, j, :, :, :, cols].reshape(total, tile),
                preferred_element_type=f32,
            )
            part += jnp.dot(
                pre_in[kv], hid[1, j, :, :, :, cols].reshape(total, tile),
                preferred_element_type=f32,
            )
            store(pl.ds(pl.multiple_of(i * tile, tile), tile), part)

    strip = 32

    def sweep(fn):
        @pl.loop(0, height // strip)
        def _(i):
            fn(pl.ds(pl.multiple_of(i * strip, strip), strip))

    def products(kv):
        def to_mate(w):
            def store(cols, part):
                mate_out[kv, w, :, cols] = part.astype(bf16)

            product(kv, w * CORES + 1 - core, store)
            start(mate_copy(kv, w))

        def to_acc(w):
            def store(cols, part):
                acc[kv, w, :, cols] = part

            product(kv, w * CORES + core, store)

        pre_copy(kv).wait_recv()
        for w in others:
            to_mate(w)
        for w in others:
            to_acc(w)
        to_mate(slot_w)
        for i, w in enumerate(others):
            mate_copy(kv, w).wait_recv()

            def fn(rows):
                v = acc[kv, w, rows, :] + mate_in[kv, w, rows, :].astype(f32)
                far_out[kv, i, rows, :] = v.astype(bf16)

            sweep(fn)
            start(far_copy(kv, i, w))
        to_acc(slot_w)

    def finish(kv):
        lanes = pl.ds(kv * HEAD_WIDTH, HEAD_WIDTH)
        mate_copy(kv, slot_w).wait_recv()
        for i, w in enumerate(others):
            wait_far(kv, i, w)

        @pl.loop(0, depth // HEAD_WIDTH)
        def _(j):
            at = pl.ds(pl.multiple_of(j * HEAD_WIDTH, HEAD_WIDTH), HEAD_WIDTH)
            v = acc[kv, slot_w, :, at] + mate_in[kv, slot_w, :, at].astype(f32)
            for w in others:
                v = v + far_in[kv, w, :, at].astype(f32)
            key_grad[at, lanes] = v[:HEAD_WIDTH, :].T
            val_grad[at, lanes] = v[HEAD_WIDTH:, :].T

    for e in range(2):
        for j in range(2):
            src = hidden.at[e, :, embed_cols(1 - side, j)]
            start(hidden_copy(1, e, j, seq, twin, seq, src, hid_send.at[next(slots)]))
    direct(0, 0)
    for kind in range(2):
        for i, w in enumerate(others):
            start(weight_copy(kind, mine, owner(w), far_w_send.at[i, kind], True))
        start(weight_copy(kind, mine, mate, mate_w_send.at[0, kind], True))
    for copy in loads:
        pltpu.make_async_copy(*copy).start()
    direct(0, 1)
    for h in range(kv_heads * group):
        for copy in own_loads(h):
            pltpu.make_async_copy(*copy).start()
    relay_hidden(0, 0)
    relay_hidden(0, 1)
    arrive(0)
    direct(1, 0)
    relay_weights()
    for copy in loads:
        pltpu.make_async_copy(*copy).wait()
    wait_weights()
    wait_rest(0, 0)
    project(0, 0)
    relay_hidden(1, 0)
    arrive(1)
    direct(1, 1)
    wait_rest(0, 1)
    project(0, 1)
    wait_rest(1, 0)
    project(1, 0)
    send_raw(0)
    relay_hidden(1, 1)
    for h in range(kv_heads * group):
        exchange(h, queries, qry, qry_send, qry_recv)
        exchange(h, out_grad, grd, grd_send, grd_recv)
    wait_rest(1, 1)
    project(1, 1)
    send_raw(1)
    for kv in range(kv_heads):
        settle(kv, 0)
        settle(kv, 1)
        attend(kv)
        start(pre_copy(kv))
        give_back(kv)
    for kv in range(kv_heads):
        products(kv)
    for kv in range(kv_heads):
        finish(kv)
        wait_back(kv)
    for copy in sends:
        copy.wait_send()


def put_kernel(*refs):
    count = len(refs) // 2
    sem = refs[-1]
    copies = [
        pltpu.make_async_copy(refs[i], refs[count + i], sem.at[i]) for i in range(count)
    ]
    for copy in copies:
        copy.start()
    for copy in copies:
        copy.wait()


def put_all(*arrays):
    return pl.pallas_call(
        put_kernel,
        out_shape=[jax.ShapeDtypeStruct(x.shape, x.dtype) for x in arrays],
        in_specs=[pl.BlockSpec(memory_space=pltpu.VMEM)] * len(arrays),
        out_specs=[ANY] * len(arrays),
        scratch_shapes=[pltpu.SemaphoreType.DMA((len(arrays),))],
        compiler_params=pltpu.CompilerParams(vmem_limit_bytes=1 << 20),
        name="put_all",
    )(*arrays)


def local(n_seq, n_dp, hidden, queries, key_matrix, value_matrix, out_grad):
    _, stretches, tokens, embed = hidden.shape
    full = queries.shape[3]
    width = full // n_seq
    deep, kv_width = key_matrix.shape
    kv_heads = kv_width // HEAD_WIDTH
    group = width // kv_width
    wide = group * HEAD_WIDTH
    near = n_dp // CORES // 2
    quarter = embed // 4
    rows, cols = grid_of(n_seq)
    hid_sends = 4 * (2 * (rows - 1 + cols - 1) + 2 * (rows - 1) * (cols - 1)) + 4
    total = stretches * n_seq * tokens
    block = n_seq * tokens
    bf16, f32 = jnp.bfloat16, jnp.float32
    dma = pltpu.SemaphoreType.DMA
    half = HEAD_WIDTH // 2
    inverse = np.exp(
        np.arange(half, dtype=np.float32) * np.float32(-2.0 * math.log(ROPE_BASE) / HEAD_WIDTH)
    ).astype(np.float32)
    phase = np.arange(total, dtype=np.float32)[:, None] * inverse[None, :]
    cos_half, sin_half = np.cos(phase), np.sin(phase)
    cos = np.concatenate([cos_half, cos_half], axis=1).astype(np.float32)
    sin = np.concatenate([-sin_half, sin_half], axis=1).astype(np.float32)
    heads = (kv_heads, stretches, n_seq, tokens, wide)
    single = (kv_heads * group, stretches, n_seq, tokens, HEAD_WIDTH)
    height = 2 * HEAD_WIDTH
    blocks = (kv_heads, near, height, deep)
    weights = (n_dp // 2, deep, kv_width)
    raw = (kv_heads, stretches, block, HEAD_WIDTH)
    all_heads = kv_heads * group
    spare = max(near - 1, 1)
    attn_out, query_grad, key_grad, val_grad = pl.pallas_call(
        functools.partial(kernel, n_seq, n_dp, kv_heads, group, math.gcd(deep, 256)),
        out_shape=[
            pltpu.VMEM((stretches, tokens, full), bf16),
            pltpu.VMEM((stretches, tokens, full), bf16),
            pltpu.VMEM((deep, kv_width), f32),
            pltpu.VMEM((deep, kv_width), f32),
        ],
        in_specs=[ANY] * 5 + [VMEM] * 4,
        out_specs=[VMEM] * 4,
        scratch_shapes=[
            pltpu.VMEM((2, 2, stretches, n_seq, tokens, quarter), bf16),
            pltpu.VMEM(single, bf16),
            pltpu.VMEM(single, bf16),
            pltpu.VMEM(weights, bf16),
            pltpu.VMEM(weights, bf16),
            pltpu.VMEM((block, kv_width), f32),
            pltpu.VMEM((block, kv_width), f32),
            pltpu.VMEM(raw, f32),
            pltpu.VMEM(raw, f32),
            pltpu.VMEM(raw, f32),
            pltpu.VMEM(raw, bf16),
            pltpu.VMEM(raw, f32),
            pltpu.VMEM(raw, bf16),
            pltpu.VMEM((total, kv_width), bf16),
            pltpu.VMEM((total, kv_width), bf16),
            pltpu.VMEM(heads, bf16),
            pltpu.VMEM(heads, bf16),
            pltpu.VMEM((kv_heads, height, total), bf16),
            pltpu.VMEM((kv_heads, height, total), bf16),
            pltpu.VMEM((HEAD_WIDTH, total), f32),
            pltpu.VMEM((HEAD_WIDTH, total), f32),
            pltpu.VMEM(blocks, f32),
            pltpu.VMEM(blocks, bf16),
            pltpu.VMEM(blocks, bf16),
            pltpu.VMEM((kv_heads, spare, height, deep), bf16),
            pltpu.VMEM(blocks, bf16),
            dma((4,)), dma((2, all_heads)), dma((2, kv_heads)),
            dma((hid_sends,)), dma((2, stretches, 2, n_seq)),
            dma((all_heads, n_seq)), dma((all_heads, n_seq)),
            dma((all_heads, n_seq)), dma((all_heads, n_seq)),
            dma((spare, 2)), dma((near, 2)), dma((n_dp // 2, 2)),
            dma((kv_heads, stretches)), dma((kv_heads, stretches)),
            dma((kv_heads, stretches)), dma((kv_heads, stretches)),
            dma((kv_heads,)), dma((kv_heads,)),
            dma((kv_heads, n_seq)), dma((kv_heads, n_seq)),
            dma((kv_heads, n_seq)), dma((kv_heads, n_seq)),
            dma((kv_heads, near)), dma((kv_heads, near)),
            dma((kv_heads, spare)), dma((kv_heads, near)),
        ],
        compiler_params=pltpu.CompilerParams(
            collective_id=0, has_side_effects=True, vmem_limit_bytes=VMEM_LIMIT
        ),
        name="attention_step",
    )(hidden[0], queries[0], key_matrix, value_matrix, out_grad[0],
      cos, sin, cos.T.copy(), sin.T.copy())
    attn_out, query_grad, key_grad, val_grad = put_all(
        attn_out, query_grad, key_grad, val_grad
    )
    return attn_out[None], query_grad[None], key_grad, val_grad


def solution(mesh):
    n_dp, n_seq = mesh.shape["dp"], mesh.shape["seq"]
    tokens, weights = P("dp", None, "seq", None), P("dp", "seq")
    return jax.shard_map(
        functools.partial(local, n_seq, n_dp),
        mesh=mesh,
        in_specs=(tokens, tokens, weights, weights, tokens),
        out_specs=(tokens, tokens, weights, weights),
        check_vma=False,
    )
```

time: 167 us -> 148 us (0.89)
  Pallas kernels: 166 us -> 147 us
    pallas_call x1, Pallas kernels: 164 us -> 145 us  [local(): pl.pallas_call(functools.partial(kernel, n_seq, n_dp, kv_heads, group, ma...]
where the time goes in v1:
time: 148 us
  Pallas kernels  147 us (99%)
    pallas_call x1, Pallas kernels, local(): pl.pallas_call(functools.partial(kernel, n_seq, n_dp, kv_heads, group, ma...  145 us

profile of v1, /device:TPU:0, one launch (start us, length us, event | category | flops | bytes accessed | tf_op | source)
XLA Modules:
  0.0 147.7 jit_solution(6798656764037199636)
XLA Ops:
  0.6 145.0 %attention_step.1 = (bf16[2,64,4096]{2,1,0:T(8,128)(2,1)S(1)}, bf16[2,64,4096]{2,1,0:T(8,128)(2,1)S(1)}, f32[1024,256]{1,0:T(8,128)S(1)}, f32[1024,256]{1,0:T(8,128)S(1)}) custom-call(bf16[2,64,8192]{2,1,0:T(8,128)(2,1)} %bitcast.5, bf16[2,64,4096]{2,1,0:T(8,128)(2,1)} %bitcast.6, bf16[1024,256]{1,0:T(8,128)(2,1)} %key_matrix.1, ...), custom_call_target="tpu_custom_call" | custom-call | tf_op jit(solution)/shard_map/attention_step/pallas_call | solution.py:527
  145.6 2.0 %put_all.1 = (bf16[2,64,4096]{2,1,0:T(8,128)(2,1)}, bf16[2,64,4096]{2,1,0:T(8,128)(2,1)}, f32[1024,256]{1,0:T(8,128)}, f32[1024,256]{1,0:T(8,128)}) custom-call(bf16[2,64,4096]{2,1,0:T(8,128)(2,1)S(1)} %get-tuple-element.12.refs_0_, bf16[2,64,4096]{2,1,0:T(8,128)(2,1)S(1)} %get-tuple-element.13.refs_1_, f32[1024,256]{1,0:T(8,128)S(1)} %get-tuple-element.14.refs_2_, ...), custom_call_target="tpu_custom_call" | custom-call | tf_op jit(solution)/shard_map/put_all/pallas_call | solution.py:484

commit v2 on v1

--- a/solution.py
+++ b/solution.py
@@ -43,9 +43,9 @@
     n_seq, n_dp, kv_heads, group, tile,
     hidden, queries, key_matrix, value_matrix, out_grad, cos, sin, cos_t, sin_t,
     attn_out, qgrad_out, key_grad, val_grad,
-    hid, qry, grd, key_all, val_all, raw_k, raw_v, own_k, own_v, out_k, out_v, in_k, in_v,
+    hid, qry, grd, key_all, val_all, sum_k, sum_v, raw_k, raw_v, raw_h, in_k, in_v,
     keys, vals, attn, qgrad, pre_t, pre_in,
-    key_acc, val_acc, acc, mate_out, mate_in, far_out, far_in,
+    key_acc, val_acc, acc, mate_acc, mate_out, mate_in, far_out, far_in,
     load_sem, own_sem, store_sem, hid_send, hid_recv, qry_send, qry_recv, grd_send, grd_recv,
     far_w_send, mate_w_send, w_recv, k_send, k_recv, v_send, v_recv, pre_send, pre_recv,
     a_send, a_recv, q_send, q_recv, mate_send, mate_recv, far_send, far_recv,
@@ -71,6 +71,21 @@
     quarter = hid.shape[-1]
     per = quarter // deep
     mine = slot_w * CORES + core
+    tokens = hid.shape[4]
+    piece_len = tokens // 2
+    is_end = jnp.logical_or(chip == 0, chip == chips - 1).astype(jnp.int32)
+
+    def turn(p):
+        if p == 0:
+            return 0, 0
+        outer = (1, p - 1) if p <= 4 else (0, p - 4)
+        inner = (0, p) if p <= 3 else (1, p - 4)
+        return tuple(is_end * a + (1 - is_end) * b for a, b in zip(outer, inner))
+
+    def stretch_of(c):
+        e, u = (c // 2, c % 2) if isinstance(c, int) else (lax.div(c, 2), lax.rem(c, 2))
+        start = u * piece_len
+        return e, pl.ds(start if isinstance(c, int) else pl.multiple_of(start, piece_len), piece_len)
 
     barrier = pltpu.get_barrier_semaphore()
     greeted = [(dp, p) for p in peers] + [(mate, seq), (twin, seq)]
@@ -90,12 +105,16 @@
         return pl.ds(pl.multiple_of((which * 2 + j) * quarter, quarter), quarter)
 
     loads = [
-        (hidden.at[:, :, embed_cols(side, j)], hid.at[0, j, :, seq], load_sem.at[j])
-        for j in range(2)
-    ] + [
-        (key_matrix, key_all.at[mine], load_sem.at[2]),
-        (value_matrix, val_all.at[mine], load_sem.at[3]),
+        (key_matrix, key_all.at[mine], load_sem.at[0]),
+        (value_matrix, val_all.at[mine], load_sem.at[1]),
     ]
+    for c in range(4):
+        e, at = stretch_of(c)
+        for j in range(2):
+            pltpu.make_async_copy(
+                hidden.at[e, at, embed_cols(side, j)], hid.at[0, j, e, seq, at],
+                hid_recv.at[0, c, j, seq],
+            ).start()
 
     def own_loads(h):
         return (
@@ -111,52 +130,51 @@
 
     slots = iter(range(hid_send.shape[0]))
 
-    def hidden_copy(slot, e, j, source, target_dp, target, src, send_sem):
+    def hidden_copy(slot, c, j, source, target_dp, target, send_sem, src=None):
+        e, at = stretch_of(c)
+        dst = hid.at[slot, j, e, source, at]
         return pltpu.make_async_remote_copy(
-            src_ref=src, dst_ref=hid.at[slot, j, e, source],
-            send_sem=send_sem, recv_sem=hid_recv.at[slot, e, j, source],
+            src_ref=dst if src is None else src, dst_ref=dst,
+            send_sem=send_sem, recv_sem=hid_recv.at[slot, c, j, source],
             device_id=(target_dp, target), device_id_type=MESH,
         )
 
-    def send_hidden(slot, e, j, source, target, own=False):
-        src = hidden.at[e, :, embed_cols(side, j)] if own else hid.at[slot, j, e, source]
-        start(hidden_copy(slot, e, j, source, dp, target, src, hid_send.at[next(slots)]))
-
-    def wait_hidden(slot, e, j, source):
-        src = hid.at[slot, j, e, source]
-        hidden_copy(slot, e, j, source, dp, source, src, hid_send.at[0]).wait_recv()
-
-    def direct(slot, e):
-        own = slot == 0
-        for first, second, j_pair in ((row_peers, col_peers, (0, 1)), (row_peers, col_peers, (1, 0))):
-            for p in first:
-                send_hidden(slot, e, j_pair[0], seq, p, own)
-            for p in second:
-                send_hidden(slot, e, j_pair[1], seq, p, own)
-
-    def relay_hidden(slot, e):
-        for p in row_peers:
-            wait_hidden(slot, e, 0, p)
+    def send_hidden(slot, c, j, source, target):
+        start(hidden_copy(slot, c, j, source, dp, target, hid_send.at[next(slots)]))
+
+    def wait_hidden(slot, c, j, source):
+        hidden_copy(slot, c, j, source, dp, source, hid_send.at[0]).wait_recv()
+
+    def direct(p):
+        slot, c = turn(p)
+        for j in range(2):
+            wait_hidden(slot, c, j, seq)
+        for j in range(2):
+            for q in row_peers:
+                send_hidden(slot, c, j, seq, q)
             for q in col_peers:
-                send_hidden(slot, e, 0, p, q)
-        for p in col_peers:
-            wait_hidden(slot, e, 1, p)
+                send_hidden(slot, c, 1 - j, seq, q)
+
+    def relay_hidden(p):
+        slot, c = turn(p)
+        for r in row_peers:
+            wait_hidden(slot, c, 0, r)
+            for q in col_peers:
+                send_hidden(slot, c, 0, r, q)
+        for r in col_peers:
+            wait_hidden(slot, c, 1, r)
             for q in row_peers:
-                send_hidden(slot, e, 1, p, q)
-
-    def wait_rest(slot, e):
-        for p in row_peers:
-            wait_hidden(slot, e, 1, p)
-        for p in col_peers:
-            wait_hidden(slot, e, 0, p)
-        for p in far_peers:
-            wait_hidden(slot, e, 0, p)
-            wait_hidden(slot, e, 1, p)
-
-    def arrive(e):
-        for j in range(2):
-            src = hid.at[1, j, e, seq]
-            hidden_copy(1, e, j, seq, twin, seq, src, hid_send.at[0]).wait_recv()
+                send_hidden(slot, c, 1, r, q)
+
+    def wait_rest(p):
+        slot, c = turn(p)
+        for r in row_peers:
+            wait_hidden(slot, c, 1, r)
+        for r in col_peers:
+            wait_hidden(slot, c, 0, r)
+        for r in far_peers:
+            wait_hidden(slot, c, 0, r)
+            wait_hidden(slot, c, 1, r)
 
     tables = (key_all, val_all)
     owns = (key_matrix, value_matrix)
@@ -198,50 +216,58 @@
                 device_id=(dp, p), device_id_type=MESH,
             ).wait_recv()
 
-    def project(slot, e):
-        raw_k[...] = jnp.zeros_like(raw_k)
-        raw_v[...] = jnp.zeros_like(raw_v)
+    def project(p):
+        slot, c = turn(p)
+        e, at_rows = stretch_of(c)
+        wait_rest(p)
+        sum_k[...] = jnp.zeros_like(sum_k)
+        sum_v[...] = jnp.zeros_like(sum_v)
 
         @pl.loop(0, 2 * per)
         def _(i):
             j, at = lax.div(i, per), lax.rem(i, per)
             cols = pl.ds(pl.multiple_of(at * deep, deep), deep)
-            rows = hid[slot, j, e, :, :, cols].reshape(block, deep)
-            raw_k[...] += jnp.dot(rows, key_all[i], preferred_element_type=f32)
-            raw_v[...] += jnp.dot(rows, val_all[i], preferred_element_type=f32)
-
+            rows = hid[slot, j, e, :, at_rows, cols].reshape(n_seq * piece_len, deep)
+            sum_k[...] += jnp.dot(rows, key_all[i], preferred_element_type=f32)
+            sum_v[...] += jnp.dot(rows, val_all[i], preferred_element_type=f32)
+
+        shape = (n_seq, piece_len, HEAD_WIDTH)
         for kv in range(kv_heads):
             lanes = pl.ds(kv * HEAD_WIDTH, HEAD_WIDTH)
-            to_k, to_v = (own_k, own_v) if slot == 0 else (out_k, out_v)
-            to_k[kv, e] = raw_k[:, lanes].astype(to_k.dtype)
-            to_v[kv, e] = raw_v[:, lanes].astype(to_v.dtype)
-
-    def raw_copies(kv, e):
+            raw_k[slot, kv, e, :, at_rows, :] = sum_k[:, lanes].reshape(shape)
+            raw_v[slot, kv, e, :, at_rows, :] = sum_v[:, lanes].reshape(shape)
+            raw_h[slot, kv, e, :, at_rows, :] = sum_v[:, lanes].reshape(shape).astype(bf16)
+        if p > 0:
+
+            @pl.when(slot == 1)
+            def _():
+                for kv in range(kv_heads):
+                    for copy in raw_copies(kv, c):
+                        copy.start()
+
+    def raw_copies(kv, c):
+        e, at = stretch_of(c)
         return [
             pltpu.make_async_remote_copy(
-                src_ref=src.at[kv, e], dst_ref=dst.at[kv, e],
-                send_sem=send_sem.at[kv, e], recv_sem=recv_sem.at[kv, e],
+                src_ref=src.at[1, kv, e, :, at], dst_ref=dst.at[kv, e, :, at],
+                send_sem=send_sem.at[kv, c], recv_sem=recv_sem.at[kv, c],
                 device_id=(twin, seq), device_id_type=MESH,
             )
             for src, dst, send_sem, recv_sem in (
-                (out_k, in_k, k_send, k_recv), (out_v, in_v, v_send, v_recv),
+                (raw_k, in_k, k_send, k_recv), (raw_h, in_v, v_send, v_recv),
             )
         ]
 
-    def send_raw(e):
-        for kv in range(kv_heads):
-            for copy in raw_copies(kv, e):
-                start(copy)
-
-    def settle(kv, e):
+    def settle(kv):
         lanes = pl.ds(kv * HEAD_WIDTH, HEAD_WIDTH)
-        rows = pl.ds(e * block, block)
-        for copy in raw_copies(kv, e):
-            copy.wait_recv()
-        raw = own_k[kv, e] + in_k[kv, e]
+        for c in range(4):
+            for copy in raw_copies(kv, c):
+                copy.wait_recv()
+        flat = (total, HEAD_WIDTH)
+        raw = raw_k[0, kv].reshape(flat) + in_k[kv].reshape(flat)
         swapped = jnp.concatenate([raw[:, half:], raw[:, :half]], axis=1)
-        keys[rows, lanes] = (raw * cos[rows, :] + swapped * sin[rows, :]).astype(bf16)
-        vals[rows, lanes] = (own_v[kv, e] + in_v[kv, e].astype(f32)).astype(bf16)
+        keys[:, lanes] = (raw * cos[...] + swapped * sin[...]).astype(bf16)
+        vals[:, lanes] = (raw_v[0, kv].reshape(flat) + in_v[kv].reshape(flat).astype(f32)).astype(bf16)
 
     scale = 1.0 / math.sqrt(HEAD_WIDTH)
     nt = (((1,), (1,)), ((), ()))
@@ -294,7 +320,7 @@
             device_id=(twin, seq), device_id_type=MESH,
         )
 
-    height, depth = acc.shape[2], acc.shape[3]
+    height, depth = acc.shape[3], deep
     results = ((attn, attn_out, a_send, a_recv), (qgrad, qgrad_out, q_send, q_recv))
 
     def own_store(kv, which):
@@ -323,147 +349,137 @@
                 ).wait_recv()
             own_store(kv, which).wait()
 
-    def mate_copy(kv, w):
+    parts = depth // tile
+
+    def mate_copy(kv, w, t):
         return pltpu.make_async_remote_copy(
-            src_ref=mate_out.at[kv, w], dst_ref=mate_in.at[kv, w],
-            send_sem=mate_send.at[kv, w], recv_sem=mate_recv.at[kv, w],
+            src_ref=mate_out.at[kv, w, t], dst_ref=mate_in.at[kv, w, t],
+            send_sem=mate_send.at[kv, w, t], recv_sem=mate_recv.at[kv, w, t],
             device_id=(mate, seq), device_id_type=MESH,
         )
 
-    def far_copy(kv, i, w):
+    def far_copy(kv, i, w, t, back=False):
+        at = w if back else slot_w
         return pltpu.make_async_remote_copy(
-            src_ref=far_out.at[kv, i], dst_ref=far_in.at[kv, slot_w],
-            send_sem=far_send.at[kv, i], recv_sem=far_recv.at[kv, slot_w],
+            src_ref=far_out.at[kv, i, t], dst_ref=far_in.at[kv, at, t],
+            send_sem=far_send.at[kv, i, t], recv_sem=far_recv.at[kv, at, t],
             device_id=(owner(w), seq), device_id_type=MESH,
         )
 
-    def wait_far(kv, i, w):
-        pltpu.make_async_remote_copy(
-            src_ref=far_out.at[kv, i], dst_ref=far_in.at[kv, w],
-            send_sem=far_send.at[kv, i], recv_sem=far_recv.at[kv, w],
-            device_id=(owner(w), seq), device_id_type=MESH,
-        ).wait_recv()
-
-    def product(kv, piece, store):
+    def part_of(pre, kv, slot, piece, t):
         j, at = lax.div(piece, per), lax.rem(piece, per)
-
-        @pl.loop(0, depth // tile)
-        def _(i):
-            cols = pl.ds(pl.multiple_of(at * depth + i * tile, tile), tile)
-            part = jnp.dot(
-                pre_t[kv], hid[0, j, :, :, :, cols].reshape(total, tile),
-                preferred_element_type=f32,
-            )
-            part += jnp.dot(
-                pre_in[kv], hid[1, j, :, :, :, cols].reshape(total, tile),
-                preferred_element_type=f32,
-            )
-            store(pl.ds(pl.multiple_of(i * tile, tile), tile), part)
-
-    strip = 32
-
-    def sweep(fn):
-        @pl.loop(0, height // strip)
-        def _(i):
-            fn(pl.ds(pl.multiple_of(i * strip, strip), strip))
-
-    def products(kv):
+        cols = pl.ds(pl.multiple_of(at * depth + t * tile, tile), tile)
+        rows = hid[slot, j, :, :, :, cols].reshape(total, tile)
+        return jnp.dot(pre[kv], rows, preferred_element_type=f32)
+
+    def own_products(kv):
+        for w in others + [slot_w]:
+            @pl.loop(0, parts)
+            def _(t):
+                mate_acc[kv, w, t] = part_of(pre_t, kv, 0, w * CORES + 1 - core, t)
+                acc[kv, w, t] = part_of(pre_t, kv, 0, w * CORES + core, t)
+
+    def twin_products(kv):
         def to_mate(w):
-            def store(cols, part):
-                mate_out[kv, w, :, cols] = part.astype(bf16)
-
-            product(kv, w * CORES + 1 - core, store)
-            start(mate_copy(kv, w))
+            @pl.loop(0, parts)
+            def _(t):
+                v = mate_acc[kv, w, t] + part_of(pre_in, kv, 1, w * CORES + 1 - core, t)
+                mate_out[kv, w, t] = v.astype(bf16)
+                mate_copy(kv, w, t).start()
 
         def to_acc(w):
-            def store(cols, part):
-                acc[kv, w, :, cols] = part
-
-            product(kv, w * CORES + core, store)
+            @pl.loop(0, parts)
+            def _(t):
+                acc[kv, w, t] += part_of(pre_in, kv, 1, w * CORES + core, t)
 
         pre_copy(kv).wait_recv()
         for w in others:
             to_mate(w)
         for w in others:
             to_acc(w)
+        for i, w in enumerate(others):
+            @pl.loop(0, parts)
+            def _(t):
+                mate_copy(kv, w, t).wait_recv()
+                v = acc[kv, w, t] + mate_in[kv, w, t].astype(f32)
+                far_out[kv, i, t] = v.astype(bf16)
+                far_copy(kv, i, w, t).start()
         to_mate(slot_w)
-        for i, w in enumerate(others):
-            mate_copy(kv, w).wait_recv()
-
-            def fn(rows):
-                v = acc[kv, w, rows, :] + mate_in[kv, w, rows, :].astype(f32)
-                far_out[kv, i, rows, :] = v.astype(bf16)
-
-            sweep(fn)
-            start(far_copy(kv, i, w))
         to_acc(slot_w)
+
+        @pl.loop(0, parts)
+        def _(t):
+            mate_copy(kv, slot_w, t).wait_recv()
+            acc[kv, slot_w, t] += mate_in[kv, slot_w, t].astype(f32)
 
     def finish(kv):
         lanes = pl.ds(kv * HEAD_WIDTH, HEAD_WIDTH)
-        mate_copy(kv, slot_w).wait_recv()
-        for i, w in enumerate(others):
-            wait_far(kv, i, w)
-
-        @pl.loop(0, depth // HEAD_WIDTH)
-        def _(j):
-            at = pl.ds(pl.multiple_of(j * HEAD_WIDTH, HEAD_WIDTH), HEAD_WIDTH)
-            v = acc[kv, slot_w, :, at] + mate_in[kv, slot_w, :, at].astype(f32)
-            for w in others:
-                v = v + far_in[kv, w, :, at].astype(f32)
+        for t in range(parts):
+            v = acc[kv, slot_w, t]
+            for i, w in enumerate(others):
+                far_copy(kv, i, w, t, True).wait_recv()
+                v = v + far_in[kv, w, t].astype(f32)
+            at = pl.ds(t * tile, tile)
             key_grad[at, lanes] = v[:HEAD_WIDTH, :].T
             val_grad[at, lanes] = v[HEAD_WIDTH:, :].T
 
-    for e in range(2):
-        for j in range(2):
-            src = hidden.at[e, :, embed_cols(1 - side, j)]
-            start(hidden_copy(1, e, j, seq, twin, seq, src, hid_send.at[next(slots)]))
-    direct(0, 0)
     for kind in range(2):
         for i, w in enumerate(others):
             start(weight_copy(kind, mine, owner(w), far_w_send.at[i, kind], True))
         start(weight_copy(kind, mine, mate, mate_w_send.at[0, kind], True))
+    for c in range(4):
+        e, at = stretch_of(c)
+        for j in range(2):
+            src = hidden.at[e, at, embed_cols(1 - side, j)]
+            start(hidden_copy(1, c, j, seq, twin, seq, hid_send.at[next(slots)], src))
     for copy in loads:
         pltpu.make_async_copy(*copy).start()
-    direct(0, 1)
+    direct(0)
     for h in range(kv_heads * group):
         for copy in own_loads(h):
             pltpu.make_async_copy(*copy).start()
-    relay_hidden(0, 0)
-    relay_hidden(0, 1)
-    arrive(0)
-    direct(1, 0)
-    relay_weights()
-    for copy in loads:
-        pltpu.make_async_copy(*copy).wait()
-    wait_weights()
-    wait_rest(0, 0)
-    project(0, 0)
-    relay_hidden(1, 0)
-    arrive(1)
-    direct(1, 1)
-    wait_rest(0, 1)
-    project(0, 1)
-    wait_rest(1, 0)
-    project(1, 0)
-    send_raw(0)
-    relay_hidden(1, 1)
+    steps = 8
+    for p in range(steps):
+        if p + 1 < steps:
+            direct(p + 1)
+        relay_hidden(p)
+        if p == 2:
+            relay_weights()
+        if p == 3:
+            for copy in loads:
+                pltpu.make_async_copy(*copy).wait()
+            wait_weights()
+            project(0)
+            project(1)
+        if p >= 3 and p + 1 < steps:
+            project(p - 1)
     for h in range(kv_heads * group):
         exchange(h, queries, qry, qry_send, qry_recv)
         exchange(h, out_grad, grd, grd_send, grd_recv)
-    wait_rest(1, 1)
-    project(1, 1)
-    send_raw(1)
+    project(steps - 2)
+    project(steps - 1)
     for kv in range(kv_heads):
-        settle(kv, 0)
-        settle(kv, 1)
+        settle(kv)
         attend(kv)
         start(pre_copy(kv))
         give_back(kv)
     for kv in range(kv_heads):
-        products(kv)
+        own_products(kv)
+        if kv > 0:
+            twin_products(kv - 1)
+    twin_products(kv_heads - 1)
     for kv in range(kv_heads):
         finish(kv)
         wait_back(kv)
+    for kv in range(kv_heads):
+        for c in range(4):
+            for copy in raw_copies(kv, c):
+                copy.wait_send()
+        for t in range(parts):
+            for w in range(near):
+                mate_copy(kv, w, t).wait_send()
+            for i, w in enumerate(others):
+                far_copy(kv, i, w, t).wait_send()
     for copy in sends:
         copy.wait_send()
 
@@ -503,7 +519,7 @@
     near = n_dp // CORES // 2
     quarter = embed // 4
     rows, cols = grid_of(n_seq)
-    hid_sends = 4 * (2 * (rows - 1 + cols - 1) + 2 * (rows - 1) * (cols - 1)) + 4
+    hid_sends = 8 * (2 * (rows - 1 + cols - 1) + 2 * (rows - 1) * (cols - 1)) + 8
     total = stretches * n_seq * tokens
     block = n_seq * tokens
     bf16, f32 = jnp.bfloat16, jnp.float32
@@ -519,13 +535,15 @@
     heads = (kv_heads, stretches, n_seq, tokens, wide)
     single = (kv_heads * group, stretches, n_seq, tokens, HEAD_WIDTH)
     height = 2 * HEAD_WIDTH
-    blocks = (kv_heads, near, height, deep)
+    tile = math.gcd(deep, 256)
+    parts = deep // tile
+    blocks = (kv_heads, near, parts, height, tile)
     weights = (n_dp // 2, deep, kv_width)
-    raw = (kv_heads, stretches, block, HEAD_WIDTH)
+    raw = (kv_heads, stretches, n_seq, tokens, HEAD_WIDTH)
     all_heads = kv_heads * group
     spare = max(near - 1, 1)
     attn_out, query_grad, key_grad, val_grad = pl.pallas_call(
-        functools.partial(kernel, n_seq, n_dp, kv_heads, group, math.gcd(deep, 256)),
+        functools.partial(kernel, n_seq, n_dp, kv_heads, group, tile),
         out_shape=[
             pltpu.VMEM((stretches, tokens, full), bf16),
             pltpu.VMEM((stretches, tokens, full), bf16),
@@ -540,12 +558,11 @@
             pltpu.VMEM(single, bf16),
             pltpu.VMEM(weights, bf16),
             pltpu.VMEM(weights, bf16),
-            pltpu.VMEM((block, kv_width), f32),
-            pltpu.VMEM((block, kv_width), f32),
-            pltpu.VMEM(raw, f32),
-            pltpu.VMEM(raw, f32),
-            pltpu.VMEM(raw, f32),
-            pltpu.VMEM(raw, bf16),
+            pltpu.VMEM((block // 2, kv_width), f32),
+            pltpu.VMEM((block // 2, kv_width), f32),
+            pltpu.VMEM((2,) + raw, f32),
+            pltpu.VMEM((2,) + raw, f32),
+            pltpu.VMEM((2,) + raw, bf16),
             pltpu.VMEM(raw, f32),
             pltpu.VMEM(raw, bf16),
             pltpu.VMEM((total, kv_width), bf16),
@@ -557,22 +574,23 @@
             pltpu.VMEM((HEAD_WIDTH, total), f32),
             pltpu.VMEM((HEAD_WIDTH, total), f32),
             pltpu.VMEM(blocks, f32),
+            pltpu.VMEM(blocks, f32),
             pltpu.VMEM(blocks, bf16),
             pltpu.VMEM(blocks, bf16),
-            pltpu.VMEM((kv_heads, spare, height, deep), bf16),
+            pltpu.VMEM((kv_heads, spare, parts, height, tile), bf16),
             pltpu.VMEM(blocks, bf16),
-            dma((4,)), dma((2, all_heads)), dma((2, kv_heads)),
-            dma((hid_sends,)), dma((2, stretches, 2, n_seq)),
+            dma((2,)), dma((2, all_heads)), dma((2, kv_heads)),
+            dma((hid_sends,)), dma((2, 4, 2, n_seq)),
             dma((all_heads, n_seq)), dma((all_heads, n_seq)),
             dma((all_heads, n_seq)), dma((all_heads, n_seq)),
             dma((spare, 2)), dma((near, 2)), dma((n_dp // 2, 2)),
-            dma((kv_heads, stretches)), dma((kv_heads, stretches)),
-            dma((kv_heads, stretches)), dma((kv_heads, stretches)),
+            dma((kv_heads, 4)), dma((kv_heads, 4)),
+            dma((kv_heads, 4)), dma((kv_heads, 4)),
             dma((kv_heads,)), dma((kv_heads,)),
             dma((kv_heads, n_seq)), dma((kv_heads, n_seq)),
             dma((kv_heads, n_seq)), dma((kv_heads, n_seq)),
-            dma((kv_heads, near)), dma((kv_heads, near)),
-            dma((kv_heads, spare)), dma((kv_heads, near)),
+            dma((kv_heads, near, parts)), dma((kv_heads, near, parts)),
+            dma((kv_heads, spare, parts)), dma((kv_heads, near, parts)),
         ],
         compiler_params=pltpu.CompilerParams(
             collective_id=0, has_side_effects=True, vmem_limit_bytes=VMEM_LIMIT

time: 148 us -> 153 us (1.034)
  Pallas kernels: 147 us -> 152 us
    pallas_call x1, Pallas kernels: 145 us -> 150 us  [local(): pl.pallas_call(functools.partial(kernel, n_seq, n_dp, kv_heads, group, ti...]
where the time goes in v2:
time: 153 us
  Pallas kernels  152 us (99%)
    pallas_call x1, Pallas kernels, local(): pl.pallas_call(functools.partial(kernel, n_seq, n_dp, kv_heads, group, ti...  150 us

profile of v2, /device:TPU:0, one launch (start us, length us, event | category | flops | bytes accessed | tf_op | source)
XLA Modules:
  0.0 153.1 jit_solution(11108541632386931537)
XLA Ops:
  0.6 150.4 %attention_step.1 = (bf16[2,64,4096]{2,1,0:T(8,128)(2,1)S(1)}, bf16[2,64,4096]{2,1,0:T(8,128)(2,1)S(1)}, f32[1024,256]{1,0:T(8,128)S(1)}, f32[1024,256]{1,0:T(8,128)S(1)}) custom-call(bf16[2,64,8192]{2,1,0:T(8,128)(2,1)} %bitcast.5, bf16[2,64,4096]{2,1,0:T(8,128)(2,1)} %bitcast.6, bf16[1024,256]{1,0:T(8,128)(2,1)} %key_matrix.1, ...), custom_call_target="tpu_custom_call" | custom-call | tf_op jit(solution)/shard_map/attention_step/pallas_call | solution.py:545
  151.1 2.0 %put_all.1 = (bf16[2,64,4096]{2,1,0:T(8,128)(2,1)}, bf16[2,64,4096]{2,1,0:T(8,128)(2,1)}, f32[1024,256]{1,0:T(8,128)}, f32[1024,256]{1,0:T(8,128)}) custom-call(bf16[2,64,4096]{2,1,0:T(8,128)(2,1)S(1)} %get-tuple-element.12.refs_0_, bf16[2,64,4096]{2,1,0:T(8,128)(2,1)S(1)} %get-tuple-element.13.refs_1_, f32[1024,256]{1,0:T(8,128)S(1)} %get-tuple-element.14.refs_2_, ...), custom_call_target="tpu_custom_call" | custom-call | tf_op jit(solution)/shard_map/put_all/pallas_call | solution.py:500

commit v3 on v2

--- a/solution.py
+++ b/solution.py
@@ -47,7 +47,7 @@
     keys, vals, attn, qgrad, pre_t, pre_in,
     key_acc, val_acc, acc, mate_acc, mate_out, mate_in, far_out, far_in,
     load_sem, own_sem, store_sem, hid_send, hid_recv, qry_send, qry_recv, grd_send, grd_recv,
-    far_w_send, mate_w_send, w_recv, k_send, k_recv, v_send, v_recv, pre_send, pre_recv,
+    far_w_send, far_w_recv, mate_w_send, w_recv, k_send, k_recv, v_send, v_recv, pre_send, pre_recv,
     a_send, a_recv, q_send, q_recv, mate_send, mate_recv, far_send, far_recv,
 ):
     f32, bf16 = jnp.float32, jnp.bfloat16
@@ -73,19 +73,10 @@
     mine = slot_w * CORES + core
     tokens = hid.shape[4]
     piece_len = tokens // 2
-    is_end = jnp.logical_or(chip == 0, chip == chips - 1).astype(jnp.int32)
-
-    def turn(p):
-        if p == 0:
-            return 0, 0
-        outer = (1, p - 1) if p <= 4 else (0, p - 4)
-        inner = (0, p) if p <= 3 else (1, p - 4)
-        return tuple(is_end * a + (1 - is_end) * b for a, b in zip(outer, inner))
+    turns = ((0, 0), (0, 1), (1, 0), (0, 2), (1, 1), (1, 2), (1, 3), (0, 3))
 
     def stretch_of(c):
-        e, u = (c // 2, c % 2) if isinstance(c, int) else (lax.div(c, 2), lax.rem(c, 2))
-        start = u * piece_len
-        return e, pl.ds(start if isinstance(c, int) else pl.multiple_of(start, piece_len), piece_len)
+        return c // 2, pl.ds(c % 2 * piece_len, piece_len)
 
     barrier = pltpu.get_barrier_semaphore()
     greeted = [(dp, p) for p in peers] + [(mate, seq), (twin, seq)]
@@ -146,7 +137,7 @@
         hidden_copy(slot, c, j, source, dp, source, hid_send.at[0]).wait_recv()
 
     def direct(p):
-        slot, c = turn(p)
+        slot, c = turns[p]
         for j in range(2):
             wait_hidden(slot, c, j, seq)
         for j in range(2):
@@ -156,7 +147,7 @@
                 send_hidden(slot, c, 1 - j, seq, q)
 
     def relay_hidden(p):
-        slot, c = turn(p)
+        slot, c = turns[p]
         for r in row_peers:
             wait_hidden(slot, c, 0, r)
             for q in col_peers:
@@ -167,7 +158,7 @@
                 send_hidden(slot, c, 1, r, q)
 
     def wait_rest(p):
-        slot, c = turn(p)
+        slot, c = turns[p]
         for r in row_peers:
             wait_hidden(slot, c, 1, r)
         for r in col_peers:
@@ -187,12 +178,22 @@
             device_id=(target_dp, seq), device_id_type=MESH,
         )
 
+    strip = deep // 4
+
+    def far_weight(kind, r, i, w, source):
+        at = pl.ds(r * strip, strip)
+        return pltpu.make_async_remote_copy(
+            src_ref=owns[kind].at[at], dst_ref=tables[kind].at[source * CORES + core, at],
+            send_sem=far_w_send.at[i, kind, r], recv_sem=far_w_recv.at[source, kind, r],
+            device_id=(owner(w), seq), device_id_type=MESH,
+        )
+
     def relay_weights():
         for i, w in enumerate(others):
             for kind in range(2):
-                piece = w * CORES + core
-                weight_copy(kind, piece, owner(w), far_w_send.at[i, kind]).wait_recv()
-                start(weight_copy(kind, piece, mate, mate_w_send.at[i + 1, kind]))
+                for r in range(4):
+                    far_weight(kind, r, i, w, w).wait_recv()
+                start(weight_copy(kind, w * CORES + core, mate, mate_w_send.at[i + 1, kind]))
 
     def wait_weights():
         for w in [slot_w] + others:
@@ -217,7 +218,7 @@
             ).wait_recv()
 
     def project(p):
-        slot, c = turn(p)
+        slot, c = turns[p]
         e, at_rows = stretch_of(c)
         wait_rest(p)
         sum_k[...] = jnp.zeros_like(sum_k)
@@ -237,13 +238,10 @@
             raw_k[slot, kv, e, :, at_rows, :] = sum_k[:, lanes].reshape(shape)
             raw_v[slot, kv, e, :, at_rows, :] = sum_v[:, lanes].reshape(shape)
             raw_h[slot, kv, e, :, at_rows, :] = sum_v[:, lanes].reshape(shape).astype(bf16)
-        if p > 0:
-
-            @pl.when(slot == 1)
-            def _():
-                for kv in range(kv_heads):
-                    for copy in raw_copies(kv, c):
-                        copy.start()
+        if slot == 1:
+            for kv in range(kv_heads):
+                for copy in raw_copies(kv, c):
+                    start(copy)
 
     def raw_copies(kv, c):
         e, at = stretch_of(c)
@@ -273,38 +271,51 @@
     nt = (((1,), (1,)), ((), ()))
     tn = (((0,), (0,)), ((), ()))
 
+    pack = 2 if group % 2 == 0 else 1
+    half_seq = n_seq // 2
+    rows_n = half_seq * tokens
+    tri_shape = (pack * rows_n, rows_n)
+    tri_row = lax.rem(lax.broadcasted_iota(jnp.int32, tri_shape, 0), rows_n)
+    tri = lax.broadcasted_iota(jnp.int32, tri_shape, 1) <= tri_row
+
     def attend(kv):
         lanes = pl.ds(kv * HEAD_WIDTH, HEAD_WIDTH)
         key_acc[...] = jnp.zeros_like(key_acc)
         val_acc[...] = jnp.zeros_like(val_acc)
 
-        @pl.loop(0, group)
+        @pl.loop(0, group // pack)
         def _(m):
-            head = pl.ds(pl.multiple_of(m * HEAD_WIDTH, HEAD_WIDTH), HEAD_WIDTH)
-            h = kv * group + m
-            wait_exchange(h, qry, qry_send, qry_recv)
-            wait_exchange(h, grd, grd_send, grd_recv)
-            for copy in own_loads(h):
-                pltpu.make_async_copy(*copy).wait()
-            for b in range(2):
-                span = (b + 1) * block
-                q = qry[h, b].reshape(block, HEAD_WIDTH)
-                g = grd[h, b].reshape(block, HEAD_WIDTH)
+            first = kv * group + m * pack
+            for n in range(pack):
+                h = first + n
+                wait_exchange(h, qry, qry_send, qry_recv)
+                wait_exchange(h, grd, grd_send, grd_recv)
+                for copy in own_loads(h):
+                    pltpu.make_async_copy(*copy).wait()
+            for b in range(4):
+                span, seqs = (b + 1) * rows_n, pl.ds(b % 2 * half_seq, half_seq)
+                flat = (pack * rows_n, HEAD_WIDTH)
+                q = qry[pl.ds(first, pack), b // 2, seqs].reshape(flat)
+                g = grd[pl.ds(first, pack), b // 2, seqs].reshape(flat)
                 k, v = keys[:span, lanes], vals[:span, lanes]
                 s = lax.dot_general(q, k, nt, preferred_element_type=f32) * scale
-                at = b * block + lax.broadcasted_iota(jnp.int32, s.shape, 0)
-                col = lax.broadcasted_iota(jnp.int32, s.shape, 1)
-                s = jnp.where(col <= at, s, -jnp.inf)
+                last = jnp.where(tri, s[:, span - rows_n:], -jnp.inf)
+                s = last if b == 0 else jnp.concatenate([s[:, :span - rows_n], last], axis=1)
                 e = jnp.exp(s - jnp.max(s, axis=1, keepdims=True))
                 p = e * (1.0 / jnp.sum(e, axis=1, keepdims=True))
                 p_half = p.astype(bf16)
                 o = jnp.dot(p_half, v, preferred_element_type=f32).astype(bf16)
-                attn[kv, b, :, :, head] = o.reshape(n_seq, block // n_seq, HEAD_WIDTH)
                 dot = jnp.sum(g.astype(f32) * o.astype(f32), axis=1, keepdims=True)
                 gp = lax.dot_general(g, v, nt, preferred_element_type=f32)
                 ds = (p * (gp - dot) * scale).astype(bf16)
                 dq = jnp.dot(ds, k, preferred_element_type=f32).astype(bf16)
-                qgrad[kv, b, :, :, head] = dq.reshape(n_seq, block // n_seq, HEAD_WIDTH)
+                for n in range(pack):
+                    start_n = pl.multiple_of((m * pack + n) * HEAD_WIDTH, HEAD_WIDTH)
+                    head = pl.ds(start_n, HEAD_WIDTH)
+                    shape = (half_seq, tokens, HEAD_WIDTH)
+                    rows = slice(n * rows_n, (n + 1) * rows_n)
+                    attn[kv, b // 2, seqs, :, head] = o[rows].reshape(shape)
+                    qgrad[kv, b // 2, seqs, :, head] = dq[rows].reshape(shape)
                 key_acc[:, :span] += lax.dot_general(q, ds, tn, preferred_element_type=f32)
                 val_acc[:, :span] += lax.dot_general(g, p_half, tn, preferred_element_type=f32)
 
@@ -423,58 +434,55 @@
             key_grad[at, lanes] = v[:HEAD_WIDTH, :].T
             val_grad[at, lanes] = v[HEAD_WIDTH:, :].T
 
-    for kind in range(2):
-        for i, w in enumerate(others):
-            start(weight_copy(kind, mine, owner(w), far_w_send.at[i, kind], True))
-        start(weight_copy(kind, mine, mate, mate_w_send.at[0, kind], True))
     for c in range(4):
         e, at = stretch_of(c)
         for j in range(2):
             src = hidden.at[e, at, embed_cols(1 - side, j)]
             start(hidden_copy(1, c, j, seq, twin, seq, hid_send.at[next(slots)], src))
+            for i, w in enumerate(others):
+                start(far_weight(c // 2, c % 2 * 2 + j, i, w, slot_w))
+    for kind in range(2):
+        start(weight_copy(kind, mine, mate, mate_w_send.at[0, kind], True))
     for copy in loads:
         pltpu.make_async_copy(*copy).start()
     direct(0)
     for h in range(kv_heads * group):
         for copy in own_loads(h):
             pltpu.make_async_copy(*copy).start()
-    steps = 8
-    for p in range(steps):
-        if p + 1 < steps:
-            direct(p + 1)
+    for p in range(5):
+        direct(p + 1)
         relay_hidden(p)
-        if p == 2:
-            relay_weights()
-        if p == 3:
-            for copy in loads:
-                pltpu.make_async_copy(*copy).wait()
-            wait_weights()
-            project(0)
-            project(1)
-        if p >= 3 and p + 1 < steps:
-            project(p - 1)
+    direct(6)
+    relay_hidden(5)
+    direct(7)
+    relay_weights()
+    for copy in loads:
+        pltpu.make_async_copy(*copy).wait()
+    wait_weights()
+    project(2)
+    project(4)
+    relay_hidden(6)
+    project(5)
+    relay_hidden(7)
     for h in range(kv_heads * group):
         exchange(h, queries, qry, qry_send, qry_recv)
         exchange(h, out_grad, grd, grd_send, grd_recv)
-    project(steps - 2)
-    project(steps - 1)
+    for p in (6, 0, 1, 3, 7):
+        project(p)
     for kv in range(kv_heads):
         settle(kv)
         attend(kv)
         start(pre_copy(kv))
-        give_back(kv)
-    for kv in range(kv_heads):
-        own_products(kv)
         if kv > 0:
             twin_products(kv - 1)
+            give_back(kv - 1)
+        own_products(kv)
+    give_back(kv_heads - 1)
     twin_products(kv_heads - 1)
     for kv in range(kv_heads):
         finish(kv)
         wait_back(kv)
     for kv in range(kv_heads):
-        for c in range(4):
-            for copy in raw_copies(kv, c):
-                copy.wait_send()
         for t in range(parts):
             for w in range(near):
                 mate_copy(kv, w, t).wait_send()
@@ -583,7 +591,7 @@
             dma((hid_sends,)), dma((2, 4, 2, n_seq)),
             dma((all_heads, n_seq)), dma((all_heads, n_seq)),
             dma((all_heads, n_seq)), dma((all_heads, n_seq)),
-            dma((spare, 2)), dma((near, 2)), dma((n_dp // 2, 2)),
+            dma((spare, 2, 4)), dma((near, 2, 4)), dma((near, 2)), dma((n_dp // 2, 2)),
             dma((kv_heads, 4)), dma((kv_heads, 4)),
             dma((kv_heads, 4)), dma((kv_heads, 4)),
             dma((kv_heads,)), dma((kv_heads,)),

time: 153 us -> 141 us (0.922)
  Pallas kernels: 152 us -> 140 us
    pallas_call x1, Pallas kernels: 150 us -> 138 us  [local(): pl.pallas_call(functools.partial(kernel, n_seq, n_dp, kv_heads, group, ti...]
where the time goes in v3:
time: 141 us
  Pallas kernels  140 us (99%)
    pallas_call x1, Pallas kernels, local(): pl.pallas_call(functools.partial(kernel, n_seq, n_dp, kv_heads, group, ti...  138 us

profile of v3, /device:TPU:0, one launch (start us, length us, event | category | flops | bytes accessed | tf_op | source)
XLA Modules:
  0.0 140.7 jit_solution(13607047110168532383)
XLA Ops:
  0.6 138.0 %attention_step.1 = (bf16[2,64,4096]{2,1,0:T(8,128)(2,1)S(1)}, bf16[2,64,4096]{2,1,0:T(8,128)(2,1)S(1)}, f32[1024,256]{1,0:T(8,128)S(1)}, f32[1024,256]{1,0:T(8,128)S(1)}) custom-call(bf16[2,64,8192]{2,1,0:T(8,128)(2,1)} %bitcast.5, bf16[2,64,4096]{2,1,0:T(8,128)(2,1)} %bitcast.6, bf16[1024,256]{1,0:T(8,128)(2,1)} %key_matrix.1, ...), custom_call_target="tpu_custom_call" | custom-call | tf_op jit(solution)/shard_map/attention_step/pallas_call | solution.py:553
  138.6 2.0 %put_all.1 = (bf16[2,64,4096]{2,1,0:T(8,128)(2,1)}, bf16[2,64,4096]{2,1,0:T(8,128)(2,1)}, f32[1024,256]{1,0:T(8,128)}, f32[1024,256]{1,0:T(8,128)}) custom-call(bf16[2,64,4096]{2,1,0:T(8,128)(2,1)S(1)} %get-tuple-element.12.refs_0_, bf16[2,64,4096]{2,1,0:T(8,128)(2,1)S(1)} %get-tuple-element.13.refs_1_, f32[1024,256]{1,0:T(8,128)S(1)} %get-tuple-element.14.refs_2_, ...), custom_call_target="tpu_custom_call" | custom-call | tf_op jit(solution)/shard_map/put_all/pallas_call | solution.py:508

commit v4 on v3

--- a/solution.py
+++ b/solution.py
@@ -16,6 +16,7 @@
 ANY = pl.BlockSpec(memory_space=pl.ANY)
 VMEM = pl.BlockSpec(memory_space=pltpu.VMEM)
 VMEM_LIMIT = 56 << 20
+TILE = 1024
 
 
 def grid_of(count):
@@ -130,21 +131,27 @@
             device_id=(target_dp, target), device_id_type=MESH,
         )
 
-    def send_hidden(slot, c, j, source, target):
-        start(hidden_copy(slot, c, j, source, dp, target, hid_send.at[next(slots)]))
+    def send_hidden(slot, c, j, source, target, src=None):
+        start(hidden_copy(slot, c, j, source, dp, target, hid_send.at[next(slots)], src))
 
     def wait_hidden(slot, c, j, source):
         hidden_copy(slot, c, j, source, dp, source, hid_send.at[0]).wait_recv()
 
     def direct(p):
         slot, c = turns[p]
-        for j in range(2):
-            wait_hidden(slot, c, j, seq)
+        e, at = stretch_of(c)
+        if slot == 1:
+            for j in range(2):
+                wait_hidden(slot, c, j, seq)
+
+        def source(j):
+            return None if slot == 1 else hidden.at[e, at, embed_cols(side, j)]
+
         for j in range(2):
             for q in row_peers:
-                send_hidden(slot, c, j, seq, q)
+                send_hidden(slot, c, j, seq, q, source(j))
             for q in col_peers:
-                send_hidden(slot, c, 1 - j, seq, q)
+                send_hidden(slot, c, 1 - j, seq, q, source(1 - j))
 
     def relay_hidden(p):
         slot, c = turns[p]
@@ -188,12 +195,11 @@
             device_id=(owner(w), seq), device_id_type=MESH,
         )
 
-    def relay_weights():
+    def relay_weights(kind):
         for i, w in enumerate(others):
-            for kind in range(2):
-                for r in range(4):
-                    far_weight(kind, r, i, w, w).wait_recv()
-                start(weight_copy(kind, w * CORES + core, mate, mate_w_send.at[i + 1, kind]))
+            for r in range(4):
+                far_weight(kind, r, i, w, w).wait_recv()
+            start(weight_copy(kind, w * CORES + core, mate, mate_w_send.at[i + 1, kind]))
 
     def wait_weights():
         for w in [slot_w] + others:
@@ -221,6 +227,9 @@
         slot, c = turns[p]
         e, at_rows = stretch_of(c)
         wait_rest(p)
+        if slot == 0:
+            for j in range(2):
+                wait_hidden(slot, c, j, seq)
         sum_k[...] = jnp.zeros_like(sum_k)
         sum_v[...] = jnp.zeros_like(sum_v)
 
@@ -278,7 +287,7 @@
     tri_row = lax.rem(lax.broadcasted_iota(jnp.int32, tri_shape, 0), rows_n)
     tri = lax.broadcasted_iota(jnp.int32, tri_shape, 1) <= tri_row
 
-    def attend(kv):
+    def attend(kv, between=None):
         lanes = pl.ds(kv * HEAD_WIDTH, HEAD_WIDTH)
         key_acc[...] = jnp.zeros_like(key_acc)
         val_acc[...] = jnp.zeros_like(val_acc)
@@ -286,6 +295,8 @@
         @pl.loop(0, group // pack)
         def _(m):
             first = kv * group + m * pack
+            if between is not None:
+                pl.when(m == group // pack - 1)(between)
             for n in range(pack):
                 h = first + n
                 wait_exchange(h, qry, qry_send, qry_recv)
@@ -321,17 +332,17 @@
 
         grown = key_acc[...]
         swapped = jnp.concatenate([grown[half:, :], grown[:half, :]], axis=0)
-        pre_t[kv, :HEAD_WIDTH, :] = (grown * cos_t[...] - swapped * sin_t[...]).astype(bf16)
-        pre_t[kv, HEAD_WIDTH:, :] = val_acc[...].astype(bf16)
-
-    def pre_copy(kv):
+        pre_t[kv, 0] = (grown * cos_t[...] - swapped * sin_t[...]).astype(bf16)
+        pre_t[kv, 1] = val_acc[...].astype(bf16)
+
+    def pre_copy(kv, u):
         return pltpu.make_async_remote_copy(
-            src_ref=pre_t.at[kv], dst_ref=pre_in.at[kv],
-            send_sem=pre_send.at[kv], recv_sem=pre_recv.at[kv],
+            src_ref=pre_t.at[kv, u], dst_ref=pre_in.at[kv, u],
+            send_sem=pre_send.at[kv, u], recv_sem=pre_recv.at[kv, u],
             device_id=(twin, seq), device_id_type=MESH,
         )
 
-    height, depth = acc.shape[3], deep
+    depth = deep
     results = ((attn, attn_out, a_send, a_recv), (qgrad, qgrad_out, q_send, q_recv))
 
     def own_store(kv, which):
@@ -362,48 +373,57 @@
 
     parts = depth // tile
 
-    def mate_copy(kv, w, t):
+    def mate_copy(kv, w, u, t):
         return pltpu.make_async_remote_copy(
-            src_ref=mate_out.at[kv, w, t], dst_ref=mate_in.at[kv, w, t],
-            send_sem=mate_send.at[kv, w, t], recv_sem=mate_recv.at[kv, w, t],
+            src_ref=mate_out.at[kv, w, u, t], dst_ref=mate_in.at[kv, w, u, t],
+            send_sem=mate_send.at[kv, w, u, t], recv_sem=mate_recv.at[kv, w, u, t],
             device_id=(mate, seq), device_id_type=MESH,
         )
 
-    def far_copy(kv, i, w, t, back=False):
+    def far_copy(kv, i, w, u, t, back=False):
         at = w if back else slot_w
         return pltpu.make_async_remote_copy(
-            src_ref=far_out.at[kv, i, t], dst_ref=far_in.at[kv, at, t],
-            send_sem=far_send.at[kv, i, t], recv_sem=far_recv.at[kv, at, t],
+            src_ref=far_out.at[kv, i, u, t], dst_ref=far_in.at[kv, at, u, t],
+            send_sem=far_send.at[kv, i, u, t], recv_sem=far_recv.at[kv, at, u, t],
             device_id=(owner(w), seq), device_id_type=MESH,
         )
 
-    def part_of(pre, kv, slot, piece, t):
+    def part_of(left, slot, piece, t):
         j, at = lax.div(piece, per), lax.rem(piece, per)
         cols = pl.ds(pl.multiple_of(at * depth + t * tile, tile), tile)
         rows = hid[slot, j, :, :, :, cols].reshape(total, tile)
-        return jnp.dot(pre[kv], rows, preferred_element_type=f32)
+        return jnp.dot(left, rows, preferred_element_type=f32)
 
     def own_products(kv):
+        left = pre_t.at[kv]
+
+        def both(piece, t):
+            return part_of(left[...].reshape(2 * HEAD_WIDTH, total), 0, piece, t)
+
         for w in others + [slot_w]:
             @pl.loop(0, parts)
             def _(t):
-                mate_acc[kv, w, t] = part_of(pre_t, kv, 0, w * CORES + 1 - core, t)
-                acc[kv, w, t] = part_of(pre_t, kv, 0, w * CORES + core, t)
-
-    def twin_products(kv):
+                out = both(w * CORES + 1 - core, t)
+                mate_acc[kv, w, 0, t] = out[:HEAD_WIDTH]
+                mate_acc[kv, w, 1, t] = out[HEAD_WIDTH:]
+                out = both(w * CORES + core, t)
+                acc[kv, w, 0, t] = out[:HEAD_WIDTH]
+                acc[kv, w, 1, t] = out[HEAD_WIDTH:]
+
+    def twin_products(kv, u):
         def to_mate(w):
             @pl.loop(0, parts)
             def _(t):
-                v = mate_acc[kv, w, t] + part_of(pre_in, kv, 1, w * CORES + 1 - core, t)
-                mate_out[kv, w, t] = v.astype(bf16)
-                mate_copy(kv, w, t).start()
+                v = mate_acc[kv, w, u, t] + part_of(pre_in[kv, u], 1, w * CORES + 1 - core, t)
+                mate_out[kv, w, u, t] = v.astype(bf16)
+                mate_copy(kv, w, u, t).start()
 
         def to_acc(w):
             @pl.loop(0, parts)
             def _(t):
-                acc[kv, w, t] += part_of(pre_in, kv, 1, w * CORES + core, t)
-
-        pre_copy(kv).wait_recv()
+                acc[kv, w, u, t] += part_of(pre_in[kv, u], 1, w * CORES + core, t)
+
+        pre_copy(kv, u).wait_recv()
         for w in others:
             to_mate(w)
         for w in others:
@@ -411,28 +431,23 @@
         for i, w in enumerate(others):
             @pl.loop(0, parts)
             def _(t):
-                mate_copy(kv, w, t).wait_recv()
-                v = acc[kv, w, t] + mate_in[kv, w, t].astype(f32)
-                far_out[kv, i, t] = v.astype(bf16)
-                far_copy(kv, i, w, t).start()
+                mate_copy(kv, w, u, t).wait_recv()
+                v = acc[kv, w, u, t] + mate_in[kv, w, u, t].astype(f32)
+                far_out[kv, i, u, t] = v.astype(bf16)
+                far_copy(kv, i, w, u, t).start()
         to_mate(slot_w)
         to_acc(slot_w)
 
-        @pl.loop(0, parts)
-        def _(t):
-            mate_copy(kv, slot_w, t).wait_recv()
-            acc[kv, slot_w, t] += mate_in[kv, slot_w, t].astype(f32)
-
-    def finish(kv):
+    def finish(kv, u):
         lanes = pl.ds(kv * HEAD_WIDTH, HEAD_WIDTH)
+        grad = val_grad if u else key_grad
         for t in range(parts):
-            v = acc[kv, slot_w, t]
+            mate_copy(kv, slot_w, u, t).wait_recv()
+            v = acc[kv, slot_w, u, t] + mate_in[kv, slot_w, u, t].astype(f32)
             for i, w in enumerate(others):
-                far_copy(kv, i, w, t, True).wait_recv()
-                v = v + far_in[kv, w, t].astype(f32)
-            at = pl.ds(t * tile, tile)
-            key_grad[at, lanes] = v[:HEAD_WIDTH, :].T
-            val_grad[at, lanes] = v[HEAD_WIDTH:, :].T
+                far_copy(kv, i, w, u, t, True).wait_recv()
+                v = v + far_in[kv, w, u, t].astype(f32)
+            grad[pl.ds(t * tile, tile), lanes] = v.T
 
     for c in range(4):
         e, at = stretch_of(c)
@@ -452,10 +467,12 @@
     for p in range(5):
         direct(p + 1)
         relay_hidden(p)
+        if p == 4:
+            relay_weights(0)
     direct(6)
     relay_hidden(5)
     direct(7)
-    relay_weights()
+    relay_weights(1)
     for copy in loads:
         pltpu.make_async_copy(*copy).wait()
     wait_weights()
@@ -471,23 +488,26 @@
         project(p)
     for kv in range(kv_heads):
         settle(kv)
-        attend(kv)
-        start(pre_copy(kv))
-        if kv > 0:
-            twin_products(kv - 1)
-            give_back(kv - 1)
+        attend(kv, functools.partial(twin_products, kv - 1, 1) if kv else None)
+        for u in (1, 0):
+            start(pre_copy(kv, u))
+        if kv:
+            twin_products(kv - 1, 0)
         own_products(kv)
-    give_back(kv_heads - 1)
-    twin_products(kv_heads - 1)
+        give_back(kv)
+    for u in (1, 0):
+        twin_products(kv_heads - 1, u)
     for kv in range(kv_heads):
-        finish(kv)
+        for u in (1, 0):
+            finish(kv, u)
         wait_back(kv)
     for kv in range(kv_heads):
-        for t in range(parts):
-            for w in range(near):
-                mate_copy(kv, w, t).wait_send()
-            for i, w in enumerate(others):
-                far_copy(kv, i, w, t).wait_send()
+        for u in range(2):
+            for t in range(parts):
+                for w in range(near):
+                    mate_copy(kv, w, u, t).wait_send()
+                for i, w in enumerate(others):
+                    far_copy(kv, i, w, u, t).wait_send()
     for copy in sends:
         copy.wait_send()
 
@@ -542,10 +562,9 @@
     sin = np.concatenate([-sin_half, sin_half], axis=1).astype(np.float32)
     heads = (kv_heads, stretches, n_seq, tokens, wide)
     single = (kv_heads * group, stretches, n_seq, tokens, HEAD_WIDTH)
-    height = 2 * HEAD_WIDTH
-    tile = math.gcd(deep, 256)
+    tile = math.gcd(deep, TILE)
     parts = deep // tile
-    blocks = (kv_heads, near, parts, height, tile)
+    blocks = (kv_heads, near, 2, parts, HEAD_WIDTH, tile)
     weights = (n_dp // 2, deep, kv_width)
     raw = (kv_heads, stretches, n_seq, tokens, HEAD_WIDTH)
     all_heads = kv_heads * group
@@ -577,15 +596,15 @@
             pltpu.VMEM((total, kv_width), bf16),
             pltpu.VMEM(heads, bf16),
             pltpu.VMEM(heads, bf16),
-            pltpu.VMEM((kv_heads, height, total), bf16),
-            pltpu.VMEM((kv_heads, height, total), bf16),
+            pltpu.VMEM((kv_heads, 2, HEAD_WIDTH, total), bf16),
+            pltpu.VMEM((kv_heads, 2, HEAD_WIDTH, total), bf16),
             pltpu.VMEM((HEAD_WIDTH, total), f32),
             pltpu.VMEM((HEAD_WIDTH, total), f32),
             pltpu.VMEM(blocks, f32),
             pltpu.VMEM(blocks, f32),
             pltpu.VMEM(blocks, bf16),
             pltpu.VMEM(blocks, bf16),
-            pltpu.VMEM((kv_heads, spare, parts, height, tile), bf16),
+            pltpu.VMEM((kv_heads, spare, 2, parts, HEAD_WIDTH, tile), bf16),
             pltpu.VMEM(blocks, bf16),
             dma((2,)), dma((2, all_heads)), dma((2, kv_heads)),
             dma((hid_sends,)), dma((2, 4, 2, n_seq)),
@@ -594,11 +613,11 @@
             dma((spare, 2, 4)), dma((near, 2, 4)), dma((near, 2)), dma((n_dp // 2, 2)),
             dma((kv_heads, 4)), dma((kv_heads, 4)),
             dma((kv_heads, 4)), dma((kv_heads, 4)),
-            dma((kv_heads,)), dma((kv_heads,)),
+            dma((kv_heads, 2)), dma((kv_heads, 2)),
             dma((kv_heads, n_seq)), dma((kv_heads, n_seq)),
             dma((kv_heads, n_seq)), dma((kv_heads, n_seq)),
-            dma((kv_heads, near, parts)), dma((kv_heads, near, parts)),
-            dma((kv_heads, spare, parts)), dma((kv_heads, near, parts)),
+            dma((kv_heads, near, 2, parts)), dma((kv_heads, near, 2, parts)),
+            dma((kv_heads, spare, 2, parts)), dma((kv_heads, near, 2, parts)),
         ],
         compiler_params=pltpu.CompilerParams(
             collective_id=0, has_side_effects=True, vmem_limit_bytes=VMEM_LIMIT

time: 141 us -> 138 us (0.979)
  Pallas kernels: 140 us -> 137 us
    pallas_call x1, Pallas kernels: 138 us -> 135 us  [local(): pl.pallas_call(functools.partial(kernel, n_seq, n_dp, kv_heads, group, ti...]
where the time goes in v4:
time: 138 us
  Pallas kernels  137 us (99%)
    pallas_call x1, Pallas kernels, local(): pl.pallas_call(functools.partial(kernel, n_seq, n_dp, kv_heads, group, ti...  135 us

profile of v4, /device:TPU:0, one launch (start us, length us, event | category | flops | bytes accessed | tf_op | source)
XLA Modules:
  0.0 138.1 jit_solution(4089693324066385405)
XLA Ops:
  0.6 135.3 %attention_step.1 = (bf16[2,64,4096]{2,1,0:T(8,128)(2,1)S(1)}, bf16[2,64,4096]{2,1,0:T(8,128)(2,1)S(1)}, f32[1024,256]{1,0:T(8,128)S(1)}, f32[1024,256]{1,0:T(8,128)S(1)}) custom-call(bf16[2,64,8192]{2,1,0:T(8,128)(2,1)} %bitcast.5, bf16[2,64,4096]{2,1,0:T(8,128)(2,1)} %bitcast.6, bf16[1024,256]{1,0:T(8,128)(2,1)} %key_matrix.1, ...), custom_call_target="tpu_custom_call" | custom-call | tf_op jit(solution)/shard_map/attention_step/pallas_call | solution.py:572
  135.9 2.0 %put_all.1 = (bf16[2,64,4096]{2,1,0:T(8,128)(2,1)}, bf16[2,64,4096]{2,1,0:T(8,128)(2,1)}, f32[1024,256]{1,0:T(8,128)}, f32[1024,256]{1,0:T(8,128)}) custom-call(bf16[2,64,4096]{2,1,0:T(8,128)(2,1)S(1)} %get-tuple-element.12.refs_0_, bf16[2,64,4096]{2,1,0:T(8,128)(2,1)S(1)} %get-tuple-element.13.refs_1_, f32[1024,256]{1,0:T(8,128)S(1)} %get-tuple-element.14.refs_2_, ...), custom_call_target="tpu_custom_call" | custom-call | tf_op jit(solution)/shard_map/put_all/pallas_call | solution.py:528

commit v5 on v4

--- a/solution.py
+++ b/solution.py
@@ -42,11 +42,12 @@
 
 def kernel(
     n_seq, n_dp, kv_heads, group, tile,
-    hidden, queries, key_matrix, value_matrix, out_grad, cos, sin, cos_t, sin_t,
+    hidden, queries, key_matrix, value_matrix, out_grad, cos_in, sin_in, cos_t_in, sin_t_in,
     attn_out, qgrad_out, key_grad, val_grad,
     hid, qry, grd, key_all, val_all, sum_k, sum_v, raw_k, raw_v, raw_h, in_k, in_v,
     keys, vals, attn, qgrad, pre_t, pre_in,
     key_acc, val_acc, acc, mate_acc, mate_out, mate_in, far_out, far_in,
+    cos, sin, cos_t, sin_t,
     load_sem, own_sem, store_sem, hid_send, hid_recv, qry_send, qry_recv, grd_send, grd_recv,
     far_w_send, far_w_recv, mate_w_send, w_recv, k_send, k_recv, v_send, v_recv, pre_send, pre_recv,
     a_send, a_recv, q_send, q_recv, mate_send, mate_recv, far_send, far_recv,
@@ -99,6 +100,10 @@
     loads = [
         (key_matrix, key_all.at[mine], load_sem.at[0]),
         (value_matrix, val_all.at[mine], load_sem.at[1]),
+        (cos_in, cos, load_sem.at[2]),
+        (sin_in, sin, load_sem.at[3]),
+        (cos_t_in, cos_t, load_sem.at[4]),
+        (sin_t_in, sin_t, load_sem.at[5]),
     ]
     for c in range(4):
         e, at = stretch_of(c)
@@ -489,10 +494,10 @@
     for kv in range(kv_heads):
         settle(kv)
         attend(kv, functools.partial(twin_products, kv - 1, 1) if kv else None)
-        for u in (1, 0):
-            start(pre_copy(kv, u))
+        start(pre_copy(kv, 1))
         if kv:
             twin_products(kv - 1, 0)
+        start(pre_copy(kv, 0))
         own_products(kv)
         give_back(kv)
     for u in (1, 0):
@@ -577,7 +582,7 @@
             pltpu.VMEM((deep, kv_width), f32),
             pltpu.VMEM((deep, kv_width), f32),
         ],
-        in_specs=[ANY] * 5 + [VMEM] * 4,
+        in_specs=[ANY] * 9,
         out_specs=[VMEM] * 4,
         scratch_shapes=[
             pltpu.VMEM((2, 2, stretches, n_seq, tokens, quarter), bf16),
@@ -606,7 +611,11 @@
             pltpu.VMEM(blocks, bf16),
             pltpu.VMEM((kv_heads, spare, 2, parts, HEAD_WIDTH, tile), bf16),
             pltpu.VMEM(blocks, bf16),
-            dma((2,)), dma((2, all_heads)), dma((2, kv_heads)),
+            pltpu.VMEM((total, HEAD_WIDTH), f32),
+            pltpu.VMEM((total, HEAD_WIDTH), f32),
+            pltpu.VMEM((HEAD_WIDTH, total), f32),
+            pltpu.VMEM((HEAD_WIDTH, total), f32),
+            dma((6,)), dma((2, all_heads)), dma((2, kv_heads)),
             dma((hid_sends,)), dma((2, 4, 2, n_seq)),
             dma((all_heads, n_seq)), dma((all_heads, n_seq)),
             dma((all_heads, n_seq)), dma((all_heads, n_seq)),

time: 138 us -> 137 us (level)
  no operation moved by 1% of the time
where the time goes in v5:
time: 137 us
  Pallas kernels  136 us (99%)
    pallas_call x1, Pallas kernels, local(): pl.pallas_call(functools.partial(kernel, n_seq, n_dp, kv_heads, group, ti...  134 us

profile of v5, /device:TPU:0, one launch (start us, length us, event | category | flops | bytes accessed | tf_op | source)
XLA Modules:
  0.0 137.0 jit_solution(5085238277105345986)
XLA Ops:
  0.6 134.2 %attention_step.1 = (bf16[2,64,4096]{2,1,0:T(8,128)(2,1)S(1)}, bf16[2,64,4096]{2,1,0:T(8,128)(2,1)S(1)}, f32[1024,256]{1,0:T(8,128)S(1)}, f32[1024,256]{1,0:T(8,128)S(1)}) custom-call(bf16[2,64,8192]{2,1,0:T(8,128)(2,1)} %bitcast.5, bf16[2,64,4096]{2,1,0:T(8,128)(2,1)} %bitcast.6, bf16[1024,256]{1,0:T(8,128)(2,1)} %key_matrix.1, ...), custom_call_target="tpu_custom_call" | custom-call | tf_op jit(solution)/shard_map/attention_step/pallas_call | solution.py:577
  134.8 2.0 %put_all.1 = (bf16[2,64,4096]{2,1,0:T(8,128)(2,1)}, bf16[2,64,4096]{2,1,0:T(8,128)(2,1)}, f32[1024,256]{1,0:T(8,128)}, f32[1024,256]{1,0:T(8,128)}) custom-call(bf16[2,64,4096]{2,1,0:T(8,128)(2,1)S(1)} %get-tuple-element.12.refs_0_, bf16[2,64,4096]{2,1,0:T(8,128)(2,1)S(1)} %get-tuple-element.13.refs_1_, f32[1024,256]{1,0:T(8,128)S(1)} %get-tuple-element.14.refs_2_, ...), custom_call_target="tpu_custom_call" | custom-call | tf_op jit(solution)/shard_map/put_all/pallas_call | solution.py:533

commit v6 on v5

--- a/solution.py
+++ b/solution.py
@@ -85,7 +85,6 @@
     greeted += [(owner(w), seq) for w in others]
     for device in greeted:
         pl.semaphore_signal(barrier, inc=1, device_id=device, device_id_type=MESH)
-    pl.semaphore_wait(barrier, len(greeted))
 
     def head_cols(target, kv):
         return pl.ds(pl.multiple_of(target * width + kv * wide, wide), wide)
@@ -112,6 +111,10 @@
                 hidden.at[e, at, embed_cols(side, j)], hid.at[0, j, e, seq, at],
                 hid_recv.at[0, c, j, seq],
             ).start()
+
+    for copy in loads:
+        pltpu.make_async_copy(*copy).start()
+    pl.semaphore_wait(barrier, len(greeted))
 
     def own_loads(h):
         return (
@@ -463,8 +466,6 @@
                 start(far_weight(c // 2, c % 2 * 2 + j, i, w, slot_w))
     for kind in range(2):
         start(weight_copy(kind, mine, mate, mate_w_send.at[0, kind], True))
-    for copy in loads:
-        pltpu.make_async_copy(*copy).start()
     direct(0)
     for h in range(kv_heads * group):
         for copy in own_loads(h):

time: 137 us -> 137 us (level)
  no operation moved by 1% of the time
where the time goes in v6:
time: 137 us
  Pallas kernels  136 us (99%)
    pallas_call x1, Pallas kernels, local(): pl.pallas_call(functools.partial(kernel, n_seq, n_dp, kv_heads, group, ti...  134 us

profile of v6, /device:TPU:0, one launch (start us, length us, event | category | flops | bytes accessed | tf_op | source)
XLA Modules:
  0.0 137.0 jit_solution(7056624261550704275)
XLA Ops:
  0.6 134.2 %attention_step.1 = (bf16[2,64,4096]{2,1,0:T(8,128)(2,1)S(1)}, bf16[2,64,4096]{2,1,0:T(8,128)(2,1)S(1)}, f32[1024,256]{1,0:T(8,128)S(1)}, f32[1024,256]{1,0:T(8,128)S(1)}) custom-call(bf16[2,64,8192]{2,1,0:T(8,128)(2,1)} %bitcast.5, bf16[2,64,4096]{2,1,0:T(8,128)(2,1)} %bitcast.6, bf16[1024,256]{1,0:T(8,128)(2,1)} %key_matrix.1, ...), custom_call_target="tpu_custom_call" | custom-call | tf_op jit(solution)/shard_map/attention_step/pallas_call | solution.py:578
  134.8 2.0 %put_all.1 = (bf16[2,64,4096]{2,1,0:T(8,128)(2,1)}, bf16[2,64,4096]{2,1,0:T(8,128)(2,1)}, f32[1024,256]{1,0:T(8,128)}, f32[1024,256]{1,0:T(8,128)}) custom-call(bf16[2,64,4096]{2,1,0:T(8,128)(2,1)S(1)} %get-tuple-element.12.refs_0_, bf16[2,64,4096]{2,1,0:T(8,128)(2,1)S(1)} %get-tuple-element.13.refs_1_, f32[1024,256]{1,0:T(8,128)S(1)} %get-tuple-element.14.refs_2_, ...), custom_call_target="tpu_custom_call" | custom-call | tf_op jit(solution)/shard_map/put_all/pallas_call | solution.py:534
